TPU v7x, 512 devices: a whole 4x8x8 slice. The times are simulated.
512 devices in a mesh: tx: 32 (over y, z_lo, core), ty: 16 (over z_hi, x).
Axes of the slice: x: 4, y: 8, z: 8 (z_hi: 4, z_lo: 2; z = z_hi * 2 + z_lo), core: 2. Of those that a mesh axis runs over, the one named last changes fastest.
Arguments:
- offsets: float32 [2, 64, 64, 128], P(None, 'tx', 'ty'), may hold values from 0 to 1
- circ: float32 [64, 64, 128], P('tx', 'ty'), as said below
- counts: int32 [64, 64], P('tx', 'ty'), may hold values from 1 to 128, as said below
Outputs:
- velocity: float32 [2, 64, 64, 128], P(None, 'tx', 'ty')
- moved: float32 [2, 64, 64, 128], P(None, 'tx', 'ty')
Inputs may be any that keep to these rules, and one draw needn't show every extreme that they name: counts of live slots in each cell; at least one cell holds 128; the middle quarter of the cell rows holds more on average. `circ`: circulations of order 0.02 / sqrt(128), of both signs.
All inputs are finite; a program needn't handle non-finite values.
Results may differ from a plain program's by a relative error of at most 0.00011.
Values sent between devices are 32-bit elements; how exact they have to be, the bound alone decides.
A program may use at most 64 MiB of HBM per device.

v0:
```python
import functools
import math

import jax
import jax.numpy as jnp
from jax import lax
from jax.sharding import Mesh
from jax.sharding import PartitionSpec as P

MODES = 64
TX_TY = ("tx_0", "tx_1", "tx_2", "ty_0", "ty_1")
TX = ("tx_0", "tx_1", "tx_2")
TY = ("ty_0", "ty_1")


two_pi = 2.0 * math.pi
screen = 1.5625
smooth = 0.0625
section_step = 0.25
all_shifts = ((-1, -1), (-1, 0), (-1, 1), (0, -1), (0, 0), (0, 1), (1, -1), (1, 0), (1, 1))


def over_axes(shard, axes):
    return functools.reduce(lax.psum, axes, shard)


def extended(cells, sides, width):
    for axis, dim in sides:
        count = lax.axis_size(axis)
        head = lax.slice_in_dim(cells, 0, width, axis=dim)
        tail = lax.slice_in_dim(cells, cells.shape[dim] - width, cells.shape[dim], axis=dim)
        cells = jnp.concatenate(
            [
                lax.ppermute(tail, axis, [(i, (i + 1) % count) for i in range(count)]),
                cells,
                lax.ppermute(head, axis, [((i + 1) % count, i) for i in range(count)]),
            ],
            axis=dim,
        )
    return cells


def pair_sum(target, source, shift_rows, shift_cols):
    offset_x = target[0][:, :, None] - source[0][:, None, :] - shift_cols
    offset_y = target[1][:, :, None] - source[1][:, None, :] - shift_rows
    square = offset_x * offset_x + offset_y * offset_y
    weight = source[2][:, None, :] * jnp.exp(-screen * square) / (square + smooth)
    return jnp.stack([jnp.sum(-offset_y * weight, axis=2), jnp.sum(offset_x * weight, axis=2)])


def near_row(window, shift_list):
    span_cols = window.shape[2] - 2
    target = window[:, 1, 1 : 1 + span_cols]
    summed = jnp.zeros((2,) + target.shape[1:], jnp.float32)
    for shift_rows, shift_cols in shift_list:
        source = window[:, 1 + shift_rows, 1 + shift_cols : 1 + shift_cols + span_cols]
        summed = summed + pair_sum(target, source, float(shift_rows), float(shift_cols))
    return summed


def wave_numbers():
    return (jnp.arange(MODES, dtype=jnp.int32) - MODES // 2).astype(jnp.float32)


def mode_grid(cell_count):
    wave_number = wave_numbers()
    wave_x = two_pi * wave_number[:, None] * jnp.ones((1, MODES), jnp.float32)
    wave_y = two_pi * wave_number[None, :] * jnp.ones((MODES, 1), jnp.float32)
    square = wave_x * wave_x + wave_y * wave_y
    edge_mode = wave_number == -(MODES // 2)
    zero_mode = wave_number == 0
    keep_mode = jnp.logical_not(
        edge_mode[:, None] | edge_mode[None, :] | zero_mode[:, None] & zero_mode[None, :]
    )
    safe_square = jnp.where(keep_mode, square, 1.0)
    damping = jnp.where(
        keep_mode, jnp.exp(-safe_square / (6.25 * cell_count * cell_count)) / safe_square, 0.0
    )
    return (damping, wave_x, wave_y)


def tables(coord):
    phase_angle = two_pi * wave_numbers()[:, None] * coord[None, :]
    return (jnp.cos(phase_angle), jnp.sin(phase_angle))


def contract(left_side, right_side):
    return lax.dot_general(
        left_side,
        right_side,
        (((1,), (1,)), ((), ())),
        precision=lax.Precision.HIGHEST,
        preferred_element_type=jnp.float32,
    )


def product(left_side, right_side):
    return jnp.dot(
        left_side, right_side, precision=lax.Precision.HIGHEST, preferred_element_type=jnp.float32
    )


def structure(x_position, y_position, strength):
    cos_x, sin_x = tables(x_position)
    cos_y, sin_y = tables(y_position)
    real_part = contract(strength * cos_x, cos_y) - contract(strength * sin_x, sin_y)
    imag_part = contract(strength * sin_x, cos_y) + contract(strength * cos_x, sin_y)
    return jnp.stack([real_part, imag_part])


def mode_total(x_position, y_position, strength):
    partial_modes = structure(x_position, y_position, strength.reshape(-1))
    return over_axes(partial_modes, TX_TY)


def far_velocity(x_position, y_position, scaled, wave_x, wave_y):
    cos_x, sin_x = tables(x_position)
    cos_y, sin_y = tables(y_position)
    with_imag = jnp.concatenate([wave_y * scaled[1], -wave_x * scaled[1]])
    with_real = jnp.concatenate([wave_y * scaled[0], -wave_x * scaled[0]])
    term_cos = (product(with_imag, cos_y) - product(with_real, sin_y)).reshape(2, MODES, -1)
    term_sin = (product(with_real, cos_y) + product(with_imag, sin_y)).reshape(2, MODES, -1)
    return jnp.sum(cos_x[None] * term_cos - sin_x[None] * term_sin, axis=1)


def ghost_cycle(packed):
    return extended(packed, ((TX, 1), (TY, 2)), 1)


def per_device(offsets, circ, counts):
    rows_dev, cols_dev, slot_count = circ.shape
    cell_count = rows_dev * lax.axis_size(TX)
    live_slot = jnp.arange(slot_count, dtype=jnp.int32)[None, None, :] < counts[:, :, None]
    strength = jnp.where(live_slot, circ, 0.0)
    packed = jnp.stack([offsets[0], offsets[1], strength])
    row_start = lax.axis_index(TX) * rows_dev
    col_start = lax.axis_index(TY) * cols_dev
    row_pos = (row_start + jnp.arange(rows_dev, dtype=jnp.int32)).astype(jnp.float32)
    col_pos = (col_start + jnp.arange(cols_dev, dtype=jnp.int32)).astype(jnp.float32)
    x_position = ((col_pos[None, :, None] + offsets[0]) / cell_count).reshape(-1)
    y_position = ((row_pos[:, None, None] + offsets[1]) / cell_count).reshape(-1)
    damping, wave_x, wave_y = mode_grid(cell_count)
    row_list = jnp.arange(rows_dev, dtype=jnp.int32)
    padded = ghost_cycle(packed)
    near_part = lax.map(
        lambda first_row: near_row(lax.dynamic_slice_in_dim(padded, first_row, 3, 1), all_shifts),
        row_list,
    )
    summed = mode_total(x_position, y_position, strength)
    scaled = damping[None] * summed
    near_part = jnp.transpose(near_part, (1, 0, 2, 3)) * (cell_count / two_pi)
    far_part = far_velocity(x_position, y_position, scaled, wave_x, wave_y).reshape(
        2, rows_dev, cols_dev, slot_count
    )
    velocity = jnp.where(live_slot[None], near_part + far_part, 0.0)
    moved = offsets + section_step * velocity
    return (velocity, moved)


def solution(mesh):
    torus = Mesh(mesh.devices.reshape(8, 2, 2, 4, 4), ("tx_0", "tx_1", "tx_2", "ty_0", "ty_1"))
    in_specs = (P(None, TX, TY, None), P(TX, TY, None), P(TX, TY))
    out_specs = (P(None, TX, TY, None), P(None, TX, TY, None))
    return jax.shard_map(
        per_device, mesh=torus, in_specs=in_specs, out_specs=out_specs, check_vma=False
    )
```

profile of v0, /device:TPU:64, one launch (start us, length us, event | category | flops | bytes accessed | tf_op | source)
XLA Modules:
  0.0 130.2 jit_solution(2269937825385879940)
XLA Ops:
  0.6 0.0 copy-start
  0.6 0.8 fusion.101
  1.4 0.0 copy-done
  1.4 1.9 %collective-permute-start = (f32[3,1,4,128]{3,2,1,0:T(4,128)S(1)}, f32[3,1,4,128]{3,2,1,0:T(4,128)S(1)}, u32[]{:S(2)}, u32[]{:S(2)}) collective-permute-start(f32[3,1,4,128]{3,2,1,0:T(4,128)S(1)} %get-tuple-element.161), channel_id=1, source_target_pairs={{0,16},{16,32},{32,48},{48,64},{64,80},{80,96},{96,112},{112,128},... | collective-permute-start | bytes 18440 | tf_op jit(solution)/shard_map/ppermute | solution.py:34
  3.4 3.6 %collective-permute-start.1 = (f32[3,1,4,128]{3,2,1,0:T(4,128)S(1)}, f32[3,1,4,128]{3,2,1,0:T(4,128)S(1)}, u32[]{:S(2)}, u32[]{:S(2)}) collective-permute-start(f32[3,1,4,128]{3,2,1,0:T(4,128)S(1)} %get-tuple-element.162), channel_id=1, source_target_pairs={{16,0},{32,16},{48,32},{64,48},{80,64},{96,80},{112,96},{128,112},... | collective-permute-start | bytes 18440 | tf_op jit(solution)/shard_map/ppermute | solution.py:36
  7.0 0.0 copy-start.1
  7.0 0.0 copy-start.2
  7.1 0.6 copy-done.1
  7.7 0.0 copy-done.2
  7.7 0.1 broadcast_select_fusion
  7.8 0.1 add.430
  7.9 0.1 add.422
  7.9 2.1 %fusion.57 = f32[64,64]{1,0:T(8,128)S(1)} fusion(f32[1024]{0:T(1024)S(1)} %get-tuple-element.167, f32[1024]{0:T(1024)S(1)} %bitcast.171, f32[1024]{0:T(1024)S(1)} %get-tuple-element.168, f32[64]{0:T(128)S(1)} %convert_multiply_fusion), kind=kOutput, calls=%fused_computation.137 | convolution fusion | flops 50528256 | bytes 28928 | tf_op jit(solution)/shard_map/dot_general | solution.py:88
  10.1 2.1 %fusion.58 = f32[64,64]{1,0:T(8,128)S(1)} fusion(f32[1024]{0:T(1024)S(1)} %get-tuple-element.167, f32[1024]{0:T(1024)S(1)} %bitcast.172, f32[1024]{0:T(1024)S(1)} %get-tuple-element.168, f32[64]{0:T(128)S(1)} %convert_multiply_fusion), kind=kOutput, calls=%fused_computation.138 | convolution fusion | flops 50528256 | bytes 28928 | tf_op jit(solution)/shard_map/dot_general | solution.py:88
  12.2 2.1 %fusion.53 = f32[1,64,64]{2,1,0:T(8,128)S(1)} fusion(f32[64,64]{1,0:T(8,128)S(1)} %fusion.57, f32[1024]{0:T(1024)S(1)} %get-tuple-element.167, f32[1024]{0:T(1024)S(1)} %bitcast.173, f32[1024]{0:T(1024)S(1)} %get-tuple-element.168, f32[64]{0:T(128)S(1)} %convert_multiply_fusion), kind=kOutput, calls=%fused_computation.129 | convolution fusion | flops 50532352 | bytes 45312 | tf_op jit(solution)/shard_map/dot_general | solution.py:88
  14.4 2.1 %fusion.54 = f32[1,64,64]{2,1,0:T(8,128)S(1)} fusion(f32[64,64]{1,0:T(8,128)S(1)} %fusion.58, f32[1024]{0:T(1024)S(1)} %get-tuple-element.167, f32[1024]{0:T(1024)S(1)} %bitcast.174, f32[1024]{0:T(1024)S(1)} %get-tuple-element.168, f32[64]{0:T(128)S(1)} %convert_multiply_fusion), kind=kOutput, calls=%fused_computation.131 | convolution fusion | flops 50532352 | bytes 45312 | tf_op jit(solution)/shard_map/dot_general | solution.py:88
  16.5 30.8 %psum.35 = f32[2,64,64]{2,1,0:T(8,128)S(1)} all-reduce(f32[2,64,64]{2,1,0:T(8,128)S(1)} %pad_maximum_fusion), channel_id=1, replica_groups=mesh['tx_0'=8,'tx_1'=2,'tx_2'=2,'ty_0'=4,'ty_1'=4] {'tx_0'}, use_global_device_ids=true, to_apply=%region_20.21 | all-reduce | flops 8192 | bytes 65536 | tf_op jit(solution)/shard_map/psum | solution.py:24
  47.3 11.1 %psum.36 = f32[2,64,64]{2,1,0:T(8,128)S(1)} all-reduce(f32[2,64,64]{2,1,0:T(8,128)S(1)} %psum.35), channel_id=1, replica_groups=mesh['tx_0'=8,'tx_1'=2,'tx_2'=2,'ty_0'=4,'ty_1'=4] {'tx_1'}, use_global_device_ids=true, to_apply=%region_21.22 | all-reduce | flops 8192 | bytes 65536 | tf_op jit(solution)/shard_map/psum | solution.py:24
  58.4 3.6 %psum.37 = f32[2,64,64]{2,1,0:T(8,128)S(1)} all-reduce(f32[2,64,64]{2,1,0:T(8,128)S(1)} %psum.36), channel_id=1, replica_groups=mesh['tx_0'=8,'tx_1'=2,'tx_2'=2,'ty_0'=4,'ty_1'=4] {'tx_2'}, use_global_device_ids=true, to_apply=%region_22.23 | all-reduce | flops 8192 | bytes 65536 | tf_op jit(solution)/shard_map/psum | solution.py:24
  62.0 22.9 %psum.38 = f32[2,64,64]{2,1,0:T(8,128)S(1)} all-reduce(f32[2,64,64]{2,1,0:T(8,128)S(1)} %psum.37), channel_id=1, replica_groups=mesh['tx_0'=8,'tx_1'=2,'tx_2'=2,'ty_0'=4,'ty_1'=4] {'ty_0'}, use_global_device_ids=true, to_apply=%region_23.24 | all-reduce | flops 8192 | bytes 65536 | tf_op jit(solution)/shard_map/psum | solution.py:24
  84.9 17.5 %psum.39 = f32[2,64,64]{2,1,0:T(8,128)S(1)} all-reduce(f32[2,64,64]{2,1,0:T(8,128)S(1)} %psum.38), channel_id=1, replica_groups=mesh['tx_0'=8,'tx_1'=2,'tx_2'=2,'ty_0'=4,'ty_1'=4] {'ty_1'}, use_global_device_ids=true, to_apply=%region_24.25 | all-reduce | flops 8192 | bytes 65536 | tf_op jit(solution)/shard_map/psum | solution.py:24
  102.5 0.1 divide_select_fusion
  102.6 0.1 fusion.88
  102.7 1.5 %fusion.55 = f32[128,1024]{1,0:T(8,128)S(1)} fusion(f32[1024]{0:T(1024)S(1)} %get-tuple-element.167, f32[64]{0:T(128)S(1)} %convert_multiply_fusion, f32[64,64]{1,0:T(8,128)S(1)} %get-tuple-element.157, f32[64,64]{1,0:T(8,128)S(1)} %get-tuple-element.154), kind=kOutput, calls=%fused_computation.135 | convolution fusion | flops 100737024 | bytes 561408 | tf_op jit(solution)/shard_map/dot_general | solution.py:98
  104.1 1.5 %fusion.56 = f32[128,1024]{1,0:T(8,128)S(1)} fusion(f32[1024]{0:T(1024)S(1)} %get-tuple-element.167, f32[64]{0:T(128)S(1)} %convert_multiply_fusion, f32[64,64]{1,0:T(8,128)S(1)} %get-tuple-element.158, f32[64,64]{1,0:T(8,128)S(1)} %get-tuple-element.153), kind=kOutput, calls=%fused_computation.136 | convolution fusion | flops 100737024 | bytes 561408 | tf_op jit(solution)/shard_map/dot_general | solution.py:98
  105.6 1.5 %convolution_subtract_fusion = f32[128,1024]{1,0:T(8,128)S(1)} fusion(f32[128,1024]{1,0:T(8,128)S(1)} %fusion.56, f32[1024]{0:T(1024)S(1)} %get-tuple-element.167, f32[64]{0:T(128)S(1)} %convert_multiply_fusion, f32[64,64]{1,0:T(8,128)S(1)} %get-tuple-element.157, f32[64,64]{1,0:T(8,128)S(1)} %get-tuple-element.154), kind=kOutput, calls=%fused_computation.127 | convolution fusion | flops 100868096 | bytes 1085696 | tf_op jit(solution)/shard_map/dot_general | solution.py:98
  107.1 1.0 multiply_cosine_fusion.5
  108.1 0.0 collective-permute-done
  108.1 0.0 collective-permute-done.1
  108.1 1.9 %collective-permute-start.2 = (f32[3,4,1,128]{3,2,1,0:T(1,128)S(1)}, f32[3,4,1,128]{3,2,1,0:T(1,128)S(1)}, u32[]{:S(2)}, u32[]{:S(2)}) collective-permute-start(f32[3,4,1,128]{3,2,1,0:T(1,128)S(1)} %get-tuple-element.159), channel_id=1, source_target_pairs={{0,1},{1,2},{2,3},{3,4},{4,5},{5,6},{6,7},{7,8},{8,9},{9,10},{10,1... | collective-permute-start | bytes 18440 | tf_op jit(solution)/shard_map/ppermute | solution.py:34
  110.1 8.1 %collective-permute-start.3 = (f32[3,4,1,128]{3,2,1,0:T(1,128)S(1)}, f32[3,4,1,128]{3,2,1,0:T(1,128)S(1)}, u32[]{:S(2)}, u32[]{:S(2)}) collective-permute-start(f32[3,4,1,128]{3,2,1,0:T(1,128)S(1)} %get-tuple-element.160), channel_id=1, source_target_pairs={{1,0},{2,1},{3,2},{4,3},{5,4},{6,5},{7,6},{8,7},{9,8},{10,9},{11,1... | collective-permute-start | bytes 18440 | tf_op jit(solution)/shard_map/ppermute | solution.py:36
  118.2 0.1 iota_compare_fusion
  118.3 1.5 %subtract_reduce_fusion = f32[2,1024]{1,0:T(2,128)S(1)} fusion(f32[64,1024]{1,0:T(8,128)S(1)} %get-tuple-element.166, f32[64,1024]{1,0:T(8,128)S(1)} %get-tuple-element.165, f32[128,1024]{1,0:T(8,128)S(1)} %convolution_subtract_fusion, f32[128,1024]{1,0:T(8,128)S(1)} %fusion.55, f32[1024]{0:T(1024)S(1)} %get-tuple-element.167, ...), kind=kOutput, calls=%fused_computation.132 | convolution fusion | flops 101390336 | bytes 1618176 | tf_op jit(solution)/shard_map/dot_general | solution.py:98
  119.9 0.0 collective-permute-done.2
  119.9 0.0 collective-permute-done.3
  119.9 9.7 %while.13 = (s32[]{:T(128)}, f32[2,2,4,128]{3,2,0,1:T(4,128)S(1)}, s32[2]{0:T(128)S(1)}, f32[3,4,6,128]{3,2,1,0:T(8,128)S(1)}, s32[]{:T(128)}, /*index=5*/s32[]{:T(128)}, s32[]{}, s32[]{:T(128)}, s32[]{}) while((s32[]{:T(128)}, f32[2,2,4,128]{3,2,0,1:T(4,128)S(1)}, s32[2]{0:T(128)S(1)}, f32[3,4,6,128]{3,2,1,0:T(8,128)S(1)}, s32[]{:T(128)}, ...), condition=%wide.region_19.20_spmd, body=%wide.region_0.19_spmd.sunk | while | flops 9052169 | bytes 248019 | solution.py:145
  119.9 0.6 dynamic_slice.16
  122.5 0.1 fusion.103
  122.5 1.2 multiply_reduce_fusion.15
  123.8 0.9 multiply_reduce_fusion.14
  124.8 0.6 dynamic_slice.16
  127.3 0.1 fusion.103
  127.4 1.2 multiply_reduce_fusion.15
  128.6 0.9 multiply_reduce_fusion.14
  129.6 0.6 multiply_add_fusion
  (18 shorter events, 0.2 us)
Async XLA Ops:
  0.6 0.8 copy-start
  1.4 106.7 %collective-permute-start = (f32[3,1,4,128]{3,2,1,0:T(4,128)S(1)}, f32[3,1,4,128]{3,2,1,0:T(4,128)S(1)}, u32[]{:S(2)}, u32[]{:S(2)}) collective-permute-start(f32[3,1,4,128]{3,2,1,0:T(4,128)S(1)} %get-tuple-element.161), channel_id=1, source_target_pairs={{0,16},{16,32},{32,48},{48,64},{64,80},{80,96},{96,112},{112,128},... | collective-permute-start | bytes 18440 | tf_op jit(solution)/shard_map/ppermute | solution.py:34
  3.4 104.8 %collective-permute-start.1 = (f32[3,1,4,128]{3,2,1,0:T(4,128)S(1)}, f32[3,1,4,128]{3,2,1,0:T(4,128)S(1)}, u32[]{:S(2)}, u32[]{:S(2)}) collective-permute-start(f32[3,1,4,128]{3,2,1,0:T(4,128)S(1)} %get-tuple-element.162), channel_id=1, source_target_pairs={{16,0},{32,16},{48,32},{64,48},{80,64},{96,80},{112,96},{128,112},... | collective-permute-start | bytes 18440 | tf_op jit(solution)/shard_map/ppermute | solution.py:36
  7.0 0.7 copy-start.1
  7.0 0.7 copy-start.2
  108.1 11.7 %collective-permute-start.2 = (f32[3,4,1,128]{3,2,1,0:T(1,128)S(1)}, f32[3,4,1,128]{3,2,1,0:T(1,128)S(1)}, u32[]{:S(2)}, u32[]{:S(2)}) collective-permute-start(f32[3,4,1,128]{3,2,1,0:T(1,128)S(1)} %get-tuple-element.159), channel_id=1, source_target_pairs={{0,1},{1,2},{2,3},{3,4},{4,5},{5,6},{6,7},{7,8},{8,9},{9,10},{10,1... | collective-permute-start | bytes 18440 | tf_op jit(solution)/shard_map/ppermute | solution.py:34
  110.1 9.8 %collective-permute-start.3 = (f32[3,4,1,128]{3,2,1,0:T(1,128)S(1)}, f32[3,4,1,128]{3,2,1,0:T(1,128)S(1)}, u32[]{:S(2)}, u32[]{:S(2)}) collective-permute-start(f32[3,4,1,128]{3,2,1,0:T(1,128)S(1)} %get-tuple-element.160), channel_id=1, source_target_pairs={{1,0},{2,1},{3,2},{4,3},{5,4},{6,5},{7,6},{8,7},{9,8},{10,9},{11,1... | collective-permute-start | bytes 18440 | tf_op jit(solution)/shard_map/ppermute | solution.py:36
where the time goes:
time: 131 us; the launch traced here: 130 us
  blocking collectives  85.9 us (66%)
  starting transfers between devices  15.6 us (12%)
  matrix products  14.5 us (11%)
  other arithmetic  7.21 us (6%)
  loops' own time  3.95 us (3%)
  local copies, waits for them, and re-layouts  2.15 us (2%)
    psum x5, blocking collectives, over_axes(): return functools.reduce(lax.psum, axes, shard)  85.9 us
    ppermute x2, starting transfers between devices, extended(): lax.ppermute(head, axis, [((i + 1) % count, i) for i in range(count)])  11.8 us
    dot_general x4, matrix products, contract(): lax.dot_general(left_side, right_side, (((1,), (1,)), ((), ())), precisio...  8.51 us
    dot_general x4, matrix products, product(): jnp.dot(left_side, right_side, precision=lax.Precision.HIGHEST, preferred...  5.95 us
    reduce_sum x4, other arithmetic, pair_sum(): jnp.sum(-offset_y * weight, axis=2)  4.36 us
    another operation x1, loops' own time, per_device(): lax.map(lambda first_row: near_row(lax.dynamic_slice_in_dim(padded, first...  3.95 us
    ppermute x2, starting transfers between devices, extended(): lax.ppermute(tail, axis, [(i, (i + 1) % count) for i in range(count)])  3.84 us
  transfers between devices with their start and end apart: 4, of which 0 were waited for; matrix products, arithmetic and copies ran while one was open for 12% of the time, Pallas kernels for 0%

commit v1 on v0

v1 whole, which is shorter than its diff:
```python
import math

import jax
import jax.numpy as jnp
from jax import lax
from jax.experimental import pallas as pl
from jax.experimental.pallas import tpu as pltpu
from jax.sharding import PartitionSpec as P

MESH = pl.DeviceIdType.MESH
CELLS = 64
HALF = 32
ROWS, COLS = 2, 4
TILE = ROWS * COLS
SLOTS = 128
NX, NY, NZ = 4, 8, 8
TX, TY = 32, 16

two_pi = 2.0 * math.pi
screen = 1.5625
smooth = 0.0625
section_step = 0.25
alpha = screen / math.log(2.0)
sigma = math.sqrt(alpha)
near_scale = CELLS / two_pi * sigma
directions = tuple((dr, dc) for dr in (-1, 0, 1) for dc in (-1, 0, 1) if (dr, dc) != (0, 0))


def mesh_id(x, y, z, c):
    return (y * 4 + lax.rem(z, 2) * 2 + c, lax.div(z, 2) * 4 + x)


def fan(tx, ty):
    return (
        lax.rem(ty, 4),
        lax.div(tx, 4),
        lax.div(ty, 4) * 2 + lax.rem(lax.div(tx, 2), 2),
        lax.rem(tx, 2),
    )


def cos_sin(turns):
    rest = turns - jnp.round(turns)
    half = rest * math.pi
    z = half * half
    sine = half * (
        1.0
        + z
        * (
            -1.0 / 6
            + z * (1.0 / 120 + z * (-1.0 / 5040 + z * (1.0 / 362880 + z * (-1.0 / 39916800))))
        )
    )
    cosine = 1.0 + z * (
        -0.5
        + z
        * (
            1.0 / 24
            + z
            * (-1.0 / 720 + z * (1.0 / 40320 + z * (-1.0 / 3628800 + z * (1.0 / 479001600))))
        )
    )
    return 1.0 - 2.0 * sine * sine, 2.0 * sine * cosine


def split(value):
    high = value.astype(jnp.bfloat16)
    return high, (value - high.astype(jnp.float32)).astype(jnp.bfloat16)


def mode_factors():
    lane = lax.broadcasted_iota(jnp.int32, (HALF, 128), 1)
    row = lax.broadcasted_iota(jnp.int32, (HALF, 128), 0)
    wave_n = lax.rem(lane, HALF)
    k_x = two_pi * row.astype(jnp.float32)
    k_y = two_pi * wave_n.astype(jnp.float32)
    square = k_x * k_x + k_y * k_y
    keep = jnp.logical_or(row > 0, wave_n > 0)
    safe = jnp.where(keep, square, 1.0)
    damping = jnp.where(keep, jnp.exp(safe * (-1.0 / (6.25 * CELLS * CELLS))) / safe, 0.0)
    images = jnp.where(row > 0, 2.0, 1.0) * jnp.where(wave_n > 0, 2.0, 1.0)
    damping = damping * images
    for_u = damping * k_y * jnp.where(lax.rem(lane, 64) < HALF, 1.0, -1.0)
    for_v = damping * k_x * jnp.where(lane < 64, 1.0, -1.0)
    return for_u, for_v


def halo_box(dr, dc):
    src_rows = {-1: (1, 1), 0: (1, ROWS), 1: (ROWS, 1)}[dr]
    src_cols = {-1: (1, 1), 0: (1, COLS), 1: (COLS, 1)}[dc]
    dst_rows = {-1: (ROWS + 1, 1), 0: (1, ROWS), 1: (0, 1)}[dr]
    dst_cols = {-1: (COLS + 1, 1), 0: (1, COLS), 1: (0, 1)}[dc]
    return tuple(pl.ds(*a) for a in (src_rows, src_cols, dst_rows, dst_cols))


def near_targets(row, col):
    return [
        r * COLS + c
        for r in range(ROWS)
        for c in range(COLS)
        if abs(row - 1 - r) <= 1 and abs(col - 1 - c) <= 1
    ]


def add_near(sources, target, total, cells):
    for at_x, at_y, at_s, targets in cells:
        target_x = [jnp.broadcast_to(target[t : t + 1, :], (8, SLOTS)) for t in targets]
        target_y = [
            jnp.broadcast_to(target[TILE + t : TILE + t + 1, :], (8, SLOTS)) for t in targets
        ]

        def group(g, sums, at_x=at_x, at_y=at_y, at_s=at_s, tx=target_x, ty=target_y):
            rows = pl.ds(pl.multiple_of(g * 8, 8), 8)
            source_x = jnp.broadcast_to(sources[rows, at_x : at_x + 1], (8, SLOTS))
            source_y = jnp.broadcast_to(sources[rows, at_y : at_y + 1], (8, SLOTS))
            strength = jnp.broadcast_to(sources[rows, at_s : at_s + 1], (8, SLOTS))
            out = []
            for k in range(len(tx)):
                a = tx[k] - source_x
                b = ty[k] - source_y
                q = a * a + b * b
                w = strength / (jnp.exp2(q) * (q + smooth * alpha))
                out.append(sums[2 * k] - b * w)
                out.append(sums[2 * k + 1] + a * w)
            return tuple(out)

        start = tuple(total[2 * t + i] for t in targets for i in range(2))
        sums = lax.fori_loop(0, SLOTS // 8, group, start)
        for k, t in enumerate(targets):
            total[2 * t] = sums[2 * k]
            total[2 * t + 1] = sums[2 * k + 1]


def kernel(
    off, circ, counts, velocity, moved,
    ext, own_rows, own_t, halo_rows, halo_t, total, near_uv, tab_x, tab_y, sided, factors,
    part, z_buf, y_buf, x_buf, final,
    halo_send, halo_recv, half_send, z_recv, y_send, y_recv, x_send, x_recv, down_send, down_recv,
    go,
):
    tx, ty = lax.axis_index("tx"), lax.axis_index("ty")
    x, y, z, c = fan(tx, ty)
    is_root = z == 0
    barrier = pltpu.get_barrier_semaphore()

    def greet(device):
        pl.semaphore_signal(barrier, inc=1, device_id=device, device_id_type=MESH)

    def copy(src, dst, send, recv, device):
        return pltpu.make_async_remote_copy(
            src_ref=src, dst_ref=dst, send_sem=send, recv_sem=recv,
            device_id=device, device_id_type=MESH,
        )

    neighbours = []
    for dr, dc in directions:
        n_tx, n_ty = lax.rem(tx + (TX + dr), TX), lax.rem(ty + (TY + dc), TY)
        neighbours.append((n_tx, n_ty))
        n_x, n_y, _, n_c = fan(n_tx, n_ty)
        greet(mesh_id(n_x, n_y, 0, n_c))

    @pl.when(jnp.logical_not(is_root))
    def _():
        greet(mesh_id(x, y, 0, c))

    @pl.when(is_root)
    def _():
        for up in range(NZ - 1, 0, -1):
            for core in range(2):
                greet(mesh_id(x, y, up, core))
        for k in range(1, NY):
            greet(mesh_id(x, lax.rem(y + k, NY), 0, c))
        for k in range(1, 2 * NX):
            greet(mesh_id(lax.rem(x + k // 2, NX), y, 0, lax.rem(c + k, 2)))

    row_of = lax.broadcasted_iota(jnp.int32, (TILE, SLOTS), 0)
    lane_of = lax.broadcasted_iota(jnp.int32, (TILE, SLOTS), 1)
    count = jnp.zeros((TILE, SLOTS), jnp.int32)
    for cell in range(TILE):
        count = jnp.where(row_of == cell, counts[cell], count)
    live = lane_of < count
    off_x, off_y = off[0], off[1]
    strength = jnp.where(live, circ[...], 0.0)
    cell_row = lax.div(row_of, COLS).astype(jnp.float32)
    cell_col = lax.rem(row_of, COLS).astype(jnp.float32)
    own_rows[2 * TILE : 3 * TILE, :] = strength

    wave = lax.broadcasted_iota(jnp.int32, (HALF, SLOTS), 0).astype(jnp.float32)
    first_col = (ty * COLS).astype(jnp.float32)
    first_row = (tx * ROWS).astype(jnp.float32)
    for cell in range(TILE):
        lanes = slice(cell * SLOTS, (cell + 1) * SLOTS)
        pos_x = (off[0, cell : cell + 1, :] + (first_col + cell % COLS)) * (1.0 / CELLS)
        pos_y = (off[1, cell : cell + 1, :] + (first_row + cell // COLS)) * (1.0 / CELLS)
        weight = own_rows[2 * TILE + cell : 2 * TILE + cell + 1, :]
        for at, table in enumerate(cos_sin(wave * pos_x)):
            rows = slice(at * HALF, (at + 1) * HALF)
            tab_x[rows, lanes] = table
            high, low = split(table * weight)
            sided[rows, lanes] = high
            sided[64 + at * HALF : 64 + (at + 1) * HALF, lanes] = low
        for at, table in enumerate(cos_sin(wave * pos_y)):
            high, low = split(table)
            tab_y[at * HALF : (at + 1) * HALF, lanes] = high
            tab_y[64 + at * HALF : 64 + (at + 1) * HALF, lanes] = high
            tab_y[128 + at * HALF : 128 + (at + 1) * HALF, lanes] = low
    sums = lax.dot_general(
        sided[...], tab_y[64:192, :], (((1,), (1,)), ((), ())),
        preferred_element_type=jnp.float32,
    )
    sums = sums[0:64] + sums[64:128]
    sums = sums + pltpu.roll(sums, 64, 1)
    wide = lax.broadcasted_iota(jnp.int32, (HALF, 128), 1)
    packed = jnp.where(wide < 64, sums[0:HALF], sums[HALF:64])
    part[0] = packed[0:16]
    part[1] = packed[16:32]

    def half_copy(h):
        return copy(
            part.at[h], z_buf.at[z * 2 + c], half_send.at[h], z_recv.at[z * 2 + c],
            mesh_id(x, y, 0, h),
        )

    @pl.when(jnp.logical_not(is_root))
    def _():
        pl.semaphore_wait(barrier, 2)
        for h in range(2):
            half_copy(h).start()

    for cell in range(TILE):
        ext[1 + cell // COLS, 1 + cell % COLS, 0] = off[0, cell : cell + 1, :]
        ext[1 + cell // COLS, 1 + cell % COLS, 1] = off[1, cell : cell + 1, :]
        ext[1 + cell // COLS, 1 + cell % COLS, 2] = own_rows[
            2 * TILE + cell : 2 * TILE + cell + 1, :
        ]
    own_rows[0:TILE, :] = (off_x + cell_col) * sigma
    own_rows[TILE : 2 * TILE, :] = (off_y + cell_row) * sigma
    own_t[...] = jnp.transpose(own_rows[...])
    total[...] = jnp.zeros_like(total)
    for_u, for_v = mode_factors()
    factors[0] = for_u
    factors[1] = for_v
    add_near(
        own_t, own_rows, total,
        [
            (k, TILE + k, 2 * TILE + k, near_targets(1 + k // COLS, 1 + k % COLS))
            for k in range(TILE)
        ],
    )

    other = 1 - c
    mate = copy(
        part.at[other], z_buf.at[c], half_send.at[0], z_recv.at[c], mesh_id(x, y, 0, other)
    )

    @pl.when(is_root)
    def _():
        pl.semaphore_wait(barrier, 64 + (NZ - 1) + (NY - 1) + (2 * NX - 1))
        mate.start()
        for up in range(1, NZ):
            pl.semaphore_signal(
                go, inc=1, device_id=mesh_id(x, y, up, c), device_id_type=MESH
            )

    @pl.when(jnp.logical_not(is_root))
    def _():
        pl.semaphore_wait(go, 1)

    halo = []
    for k, (dr, dc) in enumerate(directions):
        src_rows, src_cols, dst_rows, dst_cols = halo_box(dr, dc)
        halo.append(
            copy(
                ext.at[src_rows, src_cols], ext.at[dst_rows, dst_cols],
                halo_send.at[k], halo_recv.at[k], neighbours[k],
            )
        )
        halo[-1].start()

    y_copies = [
        copy(
            y_buf.at[y], y_buf.at[y], y_send.at[k], y_recv.at[y],
            mesh_id(x, lax.rem(y + k, NY), 0, c),
        )
        for k in range(1, NY)
    ]
    x_copies = [
        copy(
            x_buf.at[c * NX + x], x_buf.at[c * NX + x], x_send.at[k], x_recv.at[c * NX + x],
            mesh_id(lax.rem(x + k // 2, NX), y, 0, lax.rem(c + k, 2)),
        )
        for k in range(1, 2 * NX)
    ]
    down_copies = [
        copy(final, final, down_send.at[k], down_recv, mesh_id(x, y, k, c)) for k in range(1, NZ)
    ]

    @pl.when(is_root)
    def _():
        z_buf[c] = part[c]
        for up in range(1, NZ):
            for core in range(2):
                slot = up * 2 + core
                copy(part.at[0], z_buf.at[slot], half_send.at[0], z_recv.at[slot], (tx, ty)).wait_recv()
        copy(part.at[0], z_buf.at[other], half_send.at[0], z_recv.at[other], (tx, ty)).wait_recv()
        y_buf[y] = jnp.sum(z_buf[...], axis=0)
        for k in (4, 3, 5, 2, 6, 1, 7):
            y_copies[k - 1].start()
        for k in range(1, NY):
            slot = lax.rem(y + k, NY)
            copy(part.at[0], y_buf.at[slot], y_send.at[0], y_recv.at[slot], (tx, ty)).wait_recv()
        x_buf[c * NX + x] = jnp.sum(y_buf[...], axis=0)
        for k in (4, 5, 2, 3, 6, 7, 1):
            x_copies[k - 1].start()

    border = [
        (r, q) for r in range(ROWS + 2) for q in range(COLS + 2)
        if r in (0, ROWS + 1) or q in (0, COLS + 1)
    ]
    for sent in halo:
        sent.wait_recv()
    for k, (r, q) in enumerate(border):
        halo_rows[k : k + 1, :] = (ext[r, q, 0] + (q - 1.0)) * sigma
        halo_rows[16 + k : 17 + k, :] = (ext[r, q, 1] + (r - 1.0)) * sigma
        halo_rows[32 + k : 33 + k, :] = ext[r, q, 2]
    halo_t[...] = jnp.transpose(halo_rows[...])
    add_near(
        halo_t, own_rows, total,
        [(k, 16 + k, 32 + k, near_targets(r, q)) for k, (r, q) in enumerate(border)],
    )
    for t in range(TILE):
        for i in range(2):
            near_uv[i, t : t + 1, :] = jnp.sum(total[2 * t + i], axis=0, keepdims=True) * near_scale

    @pl.when(is_root)
    def _():
        for k in range(1, 2 * NX):
            slot = lax.rem(c + k, 2) * NX + lax.rem(x + k // 2, NX)
            copy(part.at[0], x_buf.at[slot], x_send.at[0], x_recv.at[slot], (tx, ty)).wait_recv()
        for h in range(2):
            final[h] = jnp.sum(x_buf[h * NX : (h + 1) * NX], axis=0)
        for k in range(1, NZ):
            down_copies[k - 1].start()

    @pl.when(jnp.logical_not(is_root))
    def _():
        down_copies[0].wait_recv()

    modes = jnp.concatenate([final[0], final[1]], axis=0)
    swapped = jnp.where(
        lax.rem(wide, 64) < HALF, pltpu.roll(modes, 96, 1), pltpu.roll(modes, 32, 1)
    )
    low_lanes = wide < 64

    def halves(value):
        high = value.astype(jnp.bfloat16).astype(jnp.float32)
        low = value - high
        high_r, low_r = pltpu.roll(high, 64, 1), pltpu.roll(low, 64, 1)
        first = (jnp.where(low_lanes, high, low_r), high)
        second = (jnp.where(low_lanes, high_r, low), high_r)
        return first, second

    u_cos, u_sin = halves(swapped * factors[0])
    v_sin, v_cos = halves(modes * factors[1])
    wide_part = jnp.concatenate([u_cos[0], u_sin[0], v_cos[0], v_sin[0]], axis=0)
    high_part = jnp.concatenate([u_cos[1], u_sin[1], v_cos[1], v_sin[1]], axis=0)
    left = jnp.concatenate(
        [wide_part.astype(jnp.bfloat16), high_part[:, 0:64].astype(jnp.bfloat16)], axis=1
    )
    field = jnp.dot(left, tab_y[...], preferred_element_type=jnp.float32)
    for i in range(2):
        for cell in range(TILE):
            lanes = slice(cell * SLOTS, (cell + 1) * SLOTS)
            product = field[64 * i : 64 * (i + 1), lanes] * tab_x[:, lanes]
            near_uv[i, cell : cell + 1, :] = near_uv[i, cell : cell + 1, :] + jnp.sum(
                product, axis=0, keepdims=True
            )
        result = jnp.where(live, near_uv[i], 0.0)
        velocity[i] = result
        moved[i] = off[i] + section_step * result

    for sent in halo:
        sent.wait_send()

    @pl.when(is_root)
    def _():
        mate.wait_send()
        for sent in y_copies + x_copies + down_copies:
            sent.wait_send()

    @pl.when(jnp.logical_not(is_root))
    def _():
        for h in range(2):
            half_copy(h).wait_send()


def per_device(offsets, circ, counts):
    shape = jax.ShapeDtypeStruct((2, TILE, SLOTS), jnp.float32)
    vmem = pl.BlockSpec(memory_space=pltpu.VMEM)
    f32, dma = jnp.float32, pltpu.SemaphoreType.DMA
    velocity, moved = pl.pallas_call(
        kernel,
        out_shape=(shape, shape),
        in_specs=[vmem, vmem, pl.BlockSpec(memory_space=pltpu.SMEM)],
        out_specs=(vmem, vmem),
        scratch_shapes=[
            pltpu.VMEM((ROWS + 2, COLS + 2, 3, 1, SLOTS), f32),
            pltpu.VMEM((3 * TILE, SLOTS), f32),
            pltpu.VMEM((SLOTS, 3 * TILE), f32),
            pltpu.VMEM((48, SLOTS), f32),
            pltpu.VMEM((SLOTS, 48), f32),
            pltpu.VMEM((2 * TILE, 8, SLOTS), f32),
            pltpu.VMEM((2, TILE, SLOTS), f32),
            pltpu.VMEM((64, TILE * SLOTS), f32),
            pltpu.VMEM((192, TILE * SLOTS), jnp.bfloat16),
            pltpu.VMEM((128, TILE * SLOTS), jnp.bfloat16),
            pltpu.VMEM((2, HALF, 128), f32),
            pltpu.VMEM((2, 16, 128), f32),
            pltpu.VMEM((16, 16, 128), f32),
            pltpu.VMEM((8, 16, 128), f32),
            pltpu.VMEM((8, 16, 128), f32),
            pltpu.VMEM((2, 16, 128), f32),
            dma((8,)), dma((8,)), dma((2,)), dma((16,)), dma((8,)), dma((8,)), dma((8,)),
            dma((8,)), dma((8,)), dma,
            pltpu.SemaphoreType.REGULAR,
        ],
        compiler_params=pltpu.CompilerParams(
            collective_id=0, has_side_effects=True, vmem_limit_bytes=16 << 20
        ),
    )(
        offsets.reshape(2, TILE, SLOTS), circ.reshape(TILE, SLOTS), counts.reshape(TILE)
    )
    out = (2, ROWS, COLS, SLOTS)
    return velocity.reshape(out), moved.reshape(out)


def solution(mesh):
    spec = P(None, "tx", "ty", None)
    return jax.shard_map(
        per_device,
        mesh=mesh,
        in_specs=(spec, P("tx", "ty", None), P("tx", "ty")),
        out_specs=(spec, spec),
        check_vma=False,
    )
```

time: 131 us -> 58.7 us (0.45)
  blocking collectives: 85.9 us -> 0 us
  Pallas kernels: 0 us -> 55.2 us
  starting transfers between devices: 15.6 us -> 0 us
  matrix products: 14.5 us -> 0 us
  other arithmetic: 7.21 us -> 0 us
  loops' own time: 3.95 us -> 0 us
    psum x5 -> x0, blocking collectives: 85.9 us -> none  [over_axes(): return functools.reduce(lax.psum, axes, shard)]
    pallas_call x0 -> x1, Pallas kernels: none -> 55.2 us  [per_device(): pl.pallas_call(kernel, out_shape=(shape, shape), in_specs=[vmem, vmem, pl...]
    ppermute x4 -> x0, starting transfers between devices: 15.6 us -> none  [the longest x2 11.8 us: extended(): lax.ppermute(head, axis, [((i + 1) % count, i) for i in range(count)])]
    dot_general x8 -> x0, matrix products: 14.5 us -> none  [the longest x4 8.51 us: contract(): lax.dot_general(left_side, right_side, (((1,), (1,)), ((), ())), precisio...]
    reduce_sum x4 -> x0, other arithmetic: 4.36 us -> none  [pair_sum(): jnp.sum(-offset_y * weight, axis=2)]
    another operation x1 -> x0, loops' own time: 3.95 us -> none  [per_device(): lax.map(lambda first_row: near_row(lax.dynamic_slice_in_dim(padded, first...]
  transfers between devices with their start and end apart: 4 -> 0, of which waited for: 0 -> 0; matrix products, arithmetic and copies ran while one was open for 12% -> 0% of each run, Pallas kernels for 0% -> 0%
where the time goes in v1:
time: 58.7 us; the launch traced here: 58.5 us
  Pallas kernels  55.2 us (94%)
  local copies, waits for them, and re-layouts  2.67 us (5%)
  between operations  0.65 us (1%)
    pallas_call x1, Pallas kernels, per_device(): pl.pallas_call(kernel, out_shape=(shape, shape), in_specs=[vmem, vmem, pl...  55.2 us
    unnamed x6, local copies, waits for them, and re-layouts  1.9 us

profile of v1, /device:TPU:64, one launch (start us, length us, event | category | flops | bytes accessed | tf_op | source)
XLA Modules:
  0.0 58.5 jit_solution(16860164181550553574)
XLA Ops:
  0.6 0.0 copy-start.1
  0.6 0.8 %reshape.21.counts = s32[8]{0:T(128)S(1)} reshape(s32[2,4]{1,0:T(2,128)} %param.5) | data formatting | bytes 64 | tf_op jit(solution)/shard_map/reshape | solution.py:431
  1.4 0.0 copy-done.1
  1.4 0.0 copy-start
  1.4 0.7 %copy-done = f32[2,2,4,128]{3,2,1,0:T(4,128)S(1)} copy-done((f32[2,2,4,128]{3,2,1,0:T(4,128)S(1)}, f32[2,2,4,128]{3,2,1,0:T(4,128)}, u32[]{:S(2)}) %copy-start) | copy-done | bytes 8216
  2.1 55.2 %shard_map.50 = (f32[2,8,128]{2,1,0:T(8,128)S(1)}, f32[2,8,128]{2,1,0:T(8,128)S(1)}) custom-call(f32[2,8,128]{2,1,0:T(8,128)S(1)} %bitcast.4, f32[8,128]{1,0:T(8,128)S(1)} %bitcast.7, s32[8]{0:T(128)S(1)} %reshape.21.counts), custom_call_target="tpu_custom_call" | custom-call | tf_op jit(solution)/shard_map/pallas_call | solution.py:401
  57.3 0.6 %copy.7 = f32[2,2,4,128]{3,2,1,0:T(4,128)} copy(f32[2,2,4,128]{3,2,1,0:T(4,128)S(1)} %bitcast.6) | data formatting | bytes 16384
  57.9 0.6 %copy.8 = f32[2,2,4,128]{3,2,1,0:T(4,128)} copy(f32[2,2,4,128]{3,2,1,0:T(4,128)S(1)} %bitcast.5) | data formatting | bytes 16384
Async XLA Ops:
  0.6 0.8 %copy-start.1 = (f32[2,4,128]{2,1,0:T(4,128)S(1)}, f32[2,4,128]{2,1,0:T(4,128)}, u32[]{:S(2)}) copy-start(f32[2,4,128]{2,1,0:T(4,128)} %param.4) | copy-start | bytes 12292
  1.4 0.7 %copy-start = (f32[2,2,4,128]{3,2,1,0:T(4,128)S(1)}, f32[2,2,4,128]{3,2,1,0:T(4,128)}, u32[]{:S(2)}) copy-start(f32[2,2,4,128]{3,2,1,0:T(4,128)} %param.3) | copy-start | bytes 24580

commit v2 on v1

--- a/solution.py
+++ b/solution.py
@@ -103,32 +103,29 @@
 
 
 def add_near(sources, target, total, cells):
-    for at_x, at_y, at_s, targets in cells:
-        target_x = [jnp.broadcast_to(target[t : t + 1, :], (8, SLOTS)) for t in targets]
-        target_y = [
-            jnp.broadcast_to(target[TILE + t : TILE + t + 1, :], (8, SLOTS)) for t in targets
-        ]
-
-        def group(g, sums, at_x=at_x, at_y=at_y, at_s=at_s, tx=target_x, ty=target_y):
-            rows = pl.ds(pl.multiple_of(g * 8, 8), 8)
-            source_x = jnp.broadcast_to(sources[rows, at_x : at_x + 1], (8, SLOTS))
-            source_y = jnp.broadcast_to(sources[rows, at_y : at_y + 1], (8, SLOTS))
-            strength = jnp.broadcast_to(sources[rows, at_s : at_s + 1], (8, SLOTS))
-            out = []
-            for k in range(len(tx)):
-                a = tx[k] - source_x
-                b = ty[k] - source_y
+    used = sorted({t for cell in cells for t in cell[3]})
+    target_x = {t: jnp.broadcast_to(target[t : t + 1, :], (8, SLOTS)) for t in used}
+    target_y = {t: jnp.broadcast_to(target[TILE + t : TILE + t + 1, :], (8, SLOTS)) for t in used}
+
+    def group(g, sums):
+        sums = list(sums)
+        block = sources[pl.ds(pl.multiple_of(g * 8, 8), 8), :]
+        for at_x, at_y, at_s, targets in cells:
+            source_x, source_y, strength = (
+                jnp.broadcast_to(block[:, at : at + 1], (8, SLOTS)) for at in (at_x, at_y, at_s)
+            )
+            for t in targets:
+                a = target_x[t] - source_x
+                b = target_y[t] - source_y
                 q = a * a + b * b
                 w = strength / (jnp.exp2(q) * (q + smooth * alpha))
-                out.append(sums[2 * k] - b * w)
-                out.append(sums[2 * k + 1] + a * w)
-            return tuple(out)
-
-        start = tuple(total[2 * t + i] for t in targets for i in range(2))
-        sums = lax.fori_loop(0, SLOTS // 8, group, start)
-        for k, t in enumerate(targets):
-            total[2 * t] = sums[2 * k]
-            total[2 * t + 1] = sums[2 * k + 1]
+                sums[2 * t] = sums[2 * t] - b * w
+                sums[2 * t + 1] = sums[2 * t + 1] + a * w
+        return tuple(sums)
+
+    sums = lax.fori_loop(0, SLOTS // 8, group, tuple(total[k] for k in range(2 * TILE)))
+    for k in range(2 * TILE):
+        total[k] = sums[k]
 
 
 def kernel(

time: 58.7 us -> 32.1 us (0.55)
  the two profiles are of different devices: /device:TPU:64 before, /device:TPU:1 now
where the time goes in v2:
time: 32.1 us; the launch traced here: 31.9 us
  Pallas kernels  28.6 us (89%)
  local copies, waits for them, and re-layouts  2.67 us (8%)
  between operations  0.65 us (2%)
    pallas_call x1, Pallas kernels, per_device(): pl.pallas_call(kernel, out_shape=(shape, shape), in_specs=[vmem, vmem, pl...  28.6 us
    unnamed x6, local copies, waits for them, and re-layouts  1.9 us
    reshape x1, local copies, waits for them, and re-layouts, per_device(): counts.reshape(TILE)  0.77 us

profile of v2, /device:TPU:1, one launch (start us, length us, event | category | flops | bytes accessed | tf_op | source)
XLA Modules:
  0.0 31.9 jit_solution(1656739718499221010)
XLA Ops:
  0.6 0.0 copy-start.1
  0.6 0.8 %reshape.21.counts = s32[8]{0:T(128)S(1)} reshape(s32[2,4]{1,0:T(2,128)} %param.5) | data formatting | bytes 64 | tf_op jit(solution)/shard_map/reshape | solution.py:428
  1.4 0.0 copy-done.1
  1.4 0.0 copy-start
  1.4 0.7 %copy-done = f32[2,2,4,128]{3,2,1,0:T(4,128)S(1)} copy-done((f32[2,2,4,128]{3,2,1,0:T(4,128)S(1)}, f32[2,2,4,128]{3,2,1,0:T(4,128)}, u32[]{:S(2)}) %copy-start) | copy-done | bytes 8216
  2.1 28.6 %shard_map.50 = (f32[2,8,128]{2,1,0:T(8,128)S(1)}, f32[2,8,128]{2,1,0:T(8,128)S(1)}) custom-call(f32[2,8,128]{2,1,0:T(8,128)S(1)} %bitcast.4, f32[8,128]{1,0:T(8,128)S(1)} %bitcast.7, s32[8]{0:T(128)S(1)} %reshape.21.counts), custom_call_target="tpu_custom_call" | custom-call | tf_op jit(solution)/shard_map/pallas_call | solution.py:398
  30.7 0.6 %copy.7 = f32[2,2,4,128]{3,2,1,0:T(4,128)} copy(f32[2,2,4,128]{3,2,1,0:T(4,128)S(1)} %bitcast.6) | data formatting | bytes 16384
  31.3 0.6 %copy.8 = f32[2,2,4,128]{3,2,1,0:T(4,128)} copy(f32[2,2,4,128]{3,2,1,0:T(4,128)S(1)} %bitcast.5) | data formatting | bytes 16384
Async XLA Ops:
  0.6 0.8 %copy-start.1 = (f32[2,4,128]{2,1,0:T(4,128)S(1)}, f32[2,4,128]{2,1,0:T(4,128)}, u32[]{:S(2)}) copy-start(f32[2,4,128]{2,1,0:T(4,128)} %param.4) | copy-start | bytes 12292
  1.4 0.7 %copy-start = (f32[2,2,4,128]{3,2,1,0:T(4,128)S(1)}, f32[2,2,4,128]{3,2,1,0:T(4,128)}, u32[]{:S(2)}) copy-start(f32[2,2,4,128]{3,2,1,0:T(4,128)} %param.3) | copy-start | bytes 24580

commit v3 on v2

--- a/solution.py
+++ b/solution.py
@@ -129,15 +129,21 @@
 
 
 def kernel(
-    off, circ, counts, velocity, moved,
-    ext, own_rows, own_t, halo_rows, halo_t, total, near_uv, tab_x, tab_y, sided, factors,
+    off_hbm, circ_hbm, counts_hbm, field_out,
+    off, circ, counts, ext, own_rows, own_t, halo_rows, halo_t, total, near_uv, tab_x, tab_y, sided, factors,
     part, z_buf, y_buf, x_buf, final,
     halo_send, halo_recv, half_send, z_recv, y_send, y_recv, x_send, x_recv, down_send, down_recv,
-    go,
+    go, load,
 ):
     tx, ty = lax.axis_index("tx"), lax.axis_index("ty")
     x, y, z, c = fan(tx, ty)
     is_root = z == 0
+    loads = [
+        pltpu.make_async_copy(src, dst, load.at[k])
+        for k, (src, dst) in enumerate(((counts_hbm, counts), (off_hbm, off), (circ_hbm, circ)))
+    ]
+    for started in loads:
+        started.start()
     barrier = pltpu.get_barrier_semaphore()
 
     def greet(device):
@@ -170,11 +176,13 @@
         for k in range(1, 2 * NX):
             greet(mesh_id(lax.rem(x + k // 2, NX), y, 0, lax.rem(c + k, 2)))
 
+    for started in loads:
+        started.wait()
     row_of = lax.broadcasted_iota(jnp.int32, (TILE, SLOTS), 0)
     lane_of = lax.broadcasted_iota(jnp.int32, (TILE, SLOTS), 1)
     count = jnp.zeros((TILE, SLOTS), jnp.int32)
     for cell in range(TILE):
-        count = jnp.where(row_of == cell, counts[cell], count)
+        count = jnp.where(row_of == cell, counts[cell // COLS, cell % COLS], count)
     live = lane_of < count
     off_x, off_y = off[0], off[1]
     strength = jnp.where(live, circ[...], 0.0)
@@ -343,6 +351,9 @@
     def _():
         down_copies[0].wait_recv()
 
+    field_out[2:4] = off[...]
+    field_out[4] = jnp.where(live, 1.0, 0.0)
+
     modes = jnp.concatenate([final[0], final[1]], axis=0)
     swapped = jnp.where(
         lax.rem(wide, 64) < HALF, pltpu.roll(modes, 96, 1), pltpu.roll(modes, 32, 1)
@@ -372,9 +383,7 @@
             near_uv[i, cell : cell + 1, :] = near_uv[i, cell : cell + 1, :] + jnp.sum(
                 product, axis=0, keepdims=True
             )
-        result = jnp.where(live, near_uv[i], 0.0)
-        velocity[i] = result
-        moved[i] = off[i] + section_step * result
+        field_out[i] = near_uv[i]
 
     for sent in halo:
         sent.wait_send()
@@ -392,15 +401,19 @@
 
 
 def per_device(offsets, circ, counts):
-    shape = jax.ShapeDtypeStruct((2, TILE, SLOTS), jnp.float32)
+    shape = jax.ShapeDtypeStruct((5, TILE, SLOTS), jnp.float32)
     vmem = pl.BlockSpec(memory_space=pltpu.VMEM)
     f32, dma = jnp.float32, pltpu.SemaphoreType.DMA
-    velocity, moved = pl.pallas_call(
+    hbm = pl.BlockSpec(memory_space=pltpu.HBM)
+    field = pl.pallas_call(
         kernel,
-        out_shape=(shape, shape),
-        in_specs=[vmem, vmem, pl.BlockSpec(memory_space=pltpu.SMEM)],
-        out_specs=(vmem, vmem),
+        out_shape=shape,
+        in_specs=[hbm, hbm, hbm],
+        out_specs=vmem,
         scratch_shapes=[
+            pltpu.VMEM((2, TILE, SLOTS), f32),
+            pltpu.VMEM((TILE, SLOTS), f32),
+            pltpu.SMEM((ROWS, COLS), jnp.int32),
             pltpu.VMEM((ROWS + 2, COLS + 2, 3, 1, SLOTS), f32),
             pltpu.VMEM((3 * TILE, SLOTS), f32),
             pltpu.VMEM((SLOTS, 3 * TILE), f32),
@@ -419,16 +432,20 @@
             pltpu.VMEM((2, 16, 128), f32),
             dma((8,)), dma((8,)), dma((2,)), dma((16,)), dma((8,)), dma((8,)), dma((8,)),
             dma((8,)), dma((8,)), dma,
-            pltpu.SemaphoreType.REGULAR,
+            pltpu.SemaphoreType.REGULAR, dma((3,)),
         ],
         compiler_params=pltpu.CompilerParams(
             collective_id=0, has_side_effects=True, vmem_limit_bytes=16 << 20
         ),
     )(
-        offsets.reshape(2, TILE, SLOTS), circ.reshape(TILE, SLOTS), counts.reshape(TILE)
-    )
-    out = (2, ROWS, COLS, SLOTS)
-    return velocity.reshape(out), moved.reshape(out)
+        *(
+            pltpu.with_memory_space_constraint(value, pltpu.HBM)
+            for value in (offsets.reshape(2, TILE, SLOTS), circ.reshape(TILE, SLOTS), counts)
+        )
+    )
+    field = field.reshape((5,) + circ.shape)
+    velocity = jnp.where(field[4:5] > 0.0, field[0:2], 0.0)
+    return velocity, field[2:4] + section_step * velocity
 
 
 def solution(mesh):

time: 32.1 us -> 30.2 us (0.941)
  local copies, waits for them, and re-layouts: 2.67 us -> 0.01 us
  other arithmetic: 0 us -> 0.62 us
    unnamed x6 -> x0, local copies, waits for them, and re-layouts: 1.9 us -> none
    reshape x1 -> x0, local copies, waits for them, and re-layouts: 0.77 us -> none  [per_device(): counts.reshape(TILE)]
    add x0 -> x1, other arithmetic: none -> 0.61 us  [per_device(): return (velocity, field[2:4] + section_step * velocity)]
where the time goes in v3:
time: 30.2 us; the launch traced here: 30 us
  Pallas kernels  28.8 us (95%)
  between operations  0.65 us (2%)
  other arithmetic  0.62 us (2%)
    pallas_call x1, Pallas kernels, per_device(): pl.pallas_call(kernel, out_shape=shape, in_specs=[hbm, hbm, hbm], out_spe...  28.8 us
    add x1, other arithmetic, per_device(): return (velocity, field[2:4] + section_step * velocity)  0.61 us

profile of v3, /device:TPU:1, one launch (start us, length us, event | category | flops | bytes accessed | tf_op | source)
XLA Modules:
  0.0 30.0 jit_solution(931217915434523973)
XLA Ops:
  0.6 28.8 %shard_map.50 = f32[5,8,128]{2,1,0:T(8,128)S(1)} custom-call(f32[2,8,128]{2,1,0:T(8,128)} %bitcast.7, f32[8,128]{1,0:T(8,128)} %bitcast.8, s32[2,4]{1,0:T(2,128)} %counts_hbm.1), custom_call_target="tpu_custom_call" | custom-call | tf_op jit(solution)/shard_map/pallas_call | solution.py:408
  29.4 0.6 %multiply_add_fusion = (f32[2,2,4,128]{3,2,1,0:T(4,128)}, f32[2,2,4,128]{3,2,1,0:T(4,128)}) fusion(f32[2,2,4,128]{3,2,1,0:T(4,128)S(1)} %bitcast.6, f32[2,2,4,128]{3,2,1,0:T(4,128)S(1)} %bitcast.5, pred[2,4,128]{2,1,0:T(4,128)(4,1)S(1)} %bitcast.9), kind=kLoop, calls=%fused_computation | loop fusion | flops 6144 | bytes 33792 | tf_op jit(solution)/shard_map/add | solution.py:448
  (2 shorter events, 0.0 us)

commit v4 on v3

--- a/solution.py
+++ b/solution.py
@@ -107,37 +107,48 @@
     target_x = {t: jnp.broadcast_to(target[t : t + 1, :], (8, SLOTS)) for t in used}
     target_y = {t: jnp.broadcast_to(target[TILE + t : TILE + t + 1, :], (8, SLOTS)) for t in used}
 
-    def group(g, sums):
+    at_once = 4 if sum(len(cell[3]) for cell in cells) > 20 else 8
+
+    def groups(step, sums):
         sums = list(sums)
-        block = sources[pl.ds(pl.multiple_of(g * 8, 8), 8), :]
-        for at_x, at_y, at_s, targets in cells:
-            source_x, source_y, strength = (
-                jnp.broadcast_to(block[:, at : at + 1], (8, SLOTS)) for at in (at_x, at_y, at_s)
-            )
-            for t in targets:
-                a = target_x[t] - source_x
-                b = target_y[t] - source_y
-                q = a * a + b * b
-                w = strength / (jnp.exp2(q) * (q + smooth * alpha))
-                sums[2 * t] = sums[2 * t] - b * w
-                sums[2 * t + 1] = sums[2 * t + 1] + a * w
+        for part in range(at_once):
+            first = pl.multiple_of((step * at_once + part) * 8, 8)
+            block = sources[pl.ds(first, 8), :]
+            for at_x, at_y, at_s, targets in cells:
+                source_x, source_y, strength = (
+                    jnp.broadcast_to(block[:, at : at + 1], (8, SLOTS)) for at in (at_x, at_y, at_s)
+                )
+                for t in targets:
+                    a = target_x[t] - source_x
+                    b = target_y[t] - source_y
+                    q = a * a + b * b
+                    w = strength / (jnp.exp2(q) * (q + smooth * alpha))
+                    sums[2 * t] = sums[2 * t] - b * w
+                    sums[2 * t + 1] = sums[2 * t + 1] + a * w
         return tuple(sums)
 
-    sums = lax.fori_loop(0, SLOTS // 8, group, tuple(total[k] for k in range(2 * TILE)))
+    steps = SLOTS // 8 // at_once
+    sums = lax.fori_loop(0, steps, groups, tuple(total[k] for k in range(2 * TILE)))
     for k in range(2 * TILE):
         total[k] = sums[k]
 
 
 def kernel(
     off_hbm, circ_hbm, counts_hbm, field_out,
-    off, circ, counts, ext, own_rows, own_t, halo_rows, halo_t, total, near_uv, tab_x, tab_y, sided, factors,
-    part, z_buf, y_buf, x_buf, final,
-    halo_send, halo_recv, half_send, z_recv, y_send, y_recv, x_send, x_recv, down_send, down_recv,
-    go, load,
+    off, circ, counts, ext, own_rows, own_t, halo_rows, halo_t, total, near_uv, tab_x, tab_y, sided,
+    factors, part, gathered, spread, final,
+    halo_send, halo_recv, part_send, part_recv, spread_send, spread_recv, down_send, down_recv, load,
+    go,
 ):
     tx, ty = lax.axis_index("tx"), lax.axis_index("ty")
     x, y, z, c = fan(tx, ty)
-    is_root = z == 0
+    in_plane = z == 0
+    is_root = jnp.logical_and(in_plane, c == 1)
+
+    def host_row(row):
+        return jnp.where(jnp.logical_or(row == 3, row == 5), 4, row)
+
+    is_host = jnp.logical_and(jnp.logical_and(in_plane, c == 0), host_row(y) == y)
     loads = [
         pltpu.make_async_copy(src, dst, load.at[k])
         for k, (src, dst) in enumerate(((counts_hbm, counts), (off_hbm, off), (circ_hbm, circ)))
@@ -155,26 +166,41 @@
             device_id=device, device_id_type=MESH,
         )
 
-    neighbours = []
-    for dr, dc in directions:
-        n_tx, n_ty = lax.rem(tx + (TX + dr), TX), lax.rem(ty + (TY + dc), TY)
-        neighbours.append((n_tx, n_ty))
-        n_x, n_y, _, n_c = fan(n_tx, n_ty)
-        greet(mesh_id(n_x, n_y, 0, n_c))
-
-    @pl.when(jnp.logical_not(is_root))
-    def _():
-        greet(mesh_id(x, y, 0, c))
+    neighbours = [
+        (lax.rem(tx + (TX + dr), TX), lax.rem(ty + (TY + dc), TY)) for dr, dc in directions
+    ]
+    for k, (n_tx, n_ty) in enumerate(neighbours):
+        n_x, n_y, _, _ = fan(n_tx, n_ty)
+        host = mesh_id(n_x, host_row(n_y), 0, 0)
+        if directions[k] in ((-1, 0), (1, 0)):
+            itself = jnp.logical_and(is_host, y == 4) if directions[k] == (-1, 0) else is_host
+
+            @pl.when(jnp.logical_not(itself))
+            def _(host=host):
+                greet(host)
+        else:
+            greet(host)
+
+    own_slot = (y * NZ + z) * 2 + c
+
+    @pl.when(in_plane)
+    def _():
+        def to_roots(k, carry):
+            greet(mesh_id(lax.rem(x + 1 + lax.div(k, NY), NX), lax.rem(y + k, NY), 0, 1))
+            return carry
+
+        lax.fori_loop(0, (NX - 1) * NY, to_roots, 0)
 
     @pl.when(is_root)
     def _():
-        for up in range(NZ - 1, 0, -1):
-            for core in range(2):
-                greet(mesh_id(x, y, up, core))
-        for k in range(1, NY):
-            greet(mesh_id(x, lax.rem(y + k, NY), 0, c))
-        for k in range(1, 2 * NX):
-            greet(mesh_id(lax.rem(x + k // 2, NX), y, 0, lax.rem(c + k, 2)))
+        def to_column(k, carry):
+            slot = lax.rem(own_slot + k, 2 * NY * NZ)
+            greet(
+                mesh_id(x, lax.div(slot, 2 * NZ), lax.rem(lax.div(slot, 2), NZ), lax.rem(slot, 2))
+            )
+            return carry
+
+        lax.fori_loop(1, 2 * NY * NZ, to_column, 0)
 
     for started in loads:
         started.wait()
@@ -217,27 +243,39 @@
     sums = sums + pltpu.roll(sums, 64, 1)
     wide = lax.broadcasted_iota(jnp.int32, (HALF, 128), 1)
     packed = jnp.where(wide < 64, sums[0:HALF], sums[HALF:64])
-    part[0] = packed[0:16]
-    part[1] = packed[16:32]
-
-    def half_copy(h):
-        return copy(
-            part.at[h], z_buf.at[z * 2 + c], half_send.at[h], z_recv.at[z * 2 + c],
-            mesh_id(x, y, 0, h),
-        )
-
-    @pl.when(jnp.logical_not(is_root))
-    def _():
-        pl.semaphore_wait(barrier, 2)
-        for h in range(2):
-            half_copy(h).start()
-
+    for k in range(NY):
+        part[k] = packed[4 * k : 4 * k + 4]
     for cell in range(TILE):
         ext[1 + cell // COLS, 1 + cell % COLS, 0] = off[0, cell : cell + 1, :]
         ext[1 + cell // COLS, 1 + cell % COLS, 1] = off[1, cell : cell + 1, :]
         ext[1 + cell // COLS, 1 + cell % COLS, 2] = own_rows[
             2 * TILE + cell : 2 * TILE + cell + 1, :
         ]
+
+    @pl.when(is_root)
+    def _():
+        pl.semaphore_wait(barrier, (NY - 1) + 2 * NY * (NX - 1))
+
+    def part_copy(k):
+        at = lax.rem(y + k, NY)
+        return copy(
+            part.at[at], gathered.at[own_slot], part_send.at[k], part_recv, mesh_id(x, at, 0, 1)
+        )
+
+    def send_parts():
+        for k in (4, 3, 5, 2, 6, 1, 7):
+            part_copy(k).start()
+
+    @pl.when(is_root)
+    def _():
+        send_parts()
+
+    @pl.when(jnp.logical_not(jnp.logical_or(is_root, is_host)))
+    def _():
+        pl.semaphore_wait(barrier, NY)
+        send_parts()
+        part_copy(0).start()
+
     own_rows[0:TILE, :] = (off_x + cell_col) * sigma
     own_rows[TILE : 2 * TILE, :] = (off_y + cell_row) * sigma
     own_t[...] = jnp.transpose(own_rows[...])
@@ -253,21 +291,25 @@
         ],
     )
 
-    other = 1 - c
-    mate = copy(
-        part.at[other], z_buf.at[c], half_send.at[0], z_recv.at[c], mesh_id(x, y, 0, other)
-    )
-
-    @pl.when(is_root)
-    def _():
-        pl.semaphore_wait(barrier, 64 + (NZ - 1) + (NY - 1) + (2 * NX - 1))
-        mate.start()
-        for up in range(1, NZ):
-            pl.semaphore_signal(
-                go, inc=1, device_id=mesh_id(x, y, up, c), device_id_type=MESH
-            )
-
-    @pl.when(jnp.logical_not(is_root))
+    def tell(device):
+        pl.semaphore_signal(go, inc=1, device_id=device, device_id_type=MESH)
+
+    @pl.when(is_host)
+    def _():
+        one_column = 2 * NZ * 8 - 1
+        pl.semaphore_wait(barrier, NY + jnp.where(y == 4, 3 * one_column + 1, one_column))
+        send_parts()
+        part_copy(0).start()
+        for k in range(1, 2 * NZ):
+            tell(mesh_id(x, y, k // 2, k % 2))
+
+        @pl.when(y == 4)
+        def _():
+            for k in range(2 * NZ):
+                for row in (3, 5):
+                    tell(mesh_id(x, row, k // 2, k % 2))
+
+    @pl.when(jnp.logical_not(is_host))
     def _():
         pl.semaphore_wait(go, 1)
 
@@ -282,79 +324,104 @@
         )
         halo[-1].start()
 
-    y_copies = [
-        copy(
-            y_buf.at[y], y_buf.at[y], y_send.at[k], y_recv.at[y],
-            mesh_id(x, lax.rem(y + k, NY), 0, c),
-        )
-        for k in range(1, NY)
-    ]
-    x_copies = [
-        copy(
-            x_buf.at[c * NX + x], x_buf.at[c * NX + x], x_send.at[k], x_recv.at[c * NX + x],
-            mesh_id(lax.rem(x + k // 2, NX), y, 0, lax.rem(c + k, 2)),
-        )
-        for k in range(1, 2 * NX)
-    ]
-    down_copies = [
-        copy(final, final, down_send.at[k], down_recv, mesh_id(x, y, k, c)) for k in range(1, NZ)
-    ]
+    def spread_copy(k, to_y):
+        return copy(
+            spread.at[y * NX + x], spread.at[y * NX + x], spread_send.at[to_y, k], spread_recv,
+            mesh_id(lax.rem(x + k // 2, NX), to_y, 0, lax.rem(c + k, 2)),
+        )
 
     @pl.when(is_root)
     def _():
-        z_buf[c] = part[c]
-        for up in range(1, NZ):
-            for core in range(2):
-                slot = up * 2 + core
-                copy(part.at[0], z_buf.at[slot], half_send.at[0], z_recv.at[slot], (tx, ty)).wait_recv()
-        copy(part.at[0], z_buf.at[other], half_send.at[0], z_recv.at[other], (tx, ty)).wait_recv()
-        y_buf[y] = jnp.sum(z_buf[...], axis=0)
-        for k in (4, 3, 5, 2, 6, 1, 7):
-            y_copies[k - 1].start()
-        for k in range(1, NY):
-            slot = lax.rem(y + k, NY)
-            copy(part.at[0], y_buf.at[slot], y_send.at[0], y_recv.at[slot], (tx, ty)).wait_recv()
-        x_buf[c * NX + x] = jnp.sum(y_buf[...], axis=0)
-        for k in (4, 5, 2, 3, 6, 7, 1):
-            x_copies[k - 1].start()
+        gathered[own_slot] = part[y]
+        others = pl.ds(0, 2 * NY * NZ - 1)
+        pltpu.make_async_copy(gathered.at[others], gathered.at[others], part_recv).wait()
+        spread[y * NX + x] = jnp.sum(gathered[...], axis=0)
+        for to_y in (0, 1, 2, 3, 7, 6, 5, 4):
+            for k in range(1, 2 * NX):
+                spread_copy(k, to_y).start()
+
+            @pl.when(y != to_y)
+            def _():
+                spread_copy(0, to_y).start()
 
     border = [
         (r, q) for r in range(ROWS + 2) for q in range(COLS + 2)
         if r in (0, ROWS + 1) or q in (0, COLS + 1)
     ]
-    for sent in halo:
-        sent.wait_recv()
-    for k, (r, q) in enumerate(border):
-        halo_rows[k : k + 1, :] = (ext[r, q, 0] + (q - 1.0)) * sigma
-        halo_rows[16 + k : 17 + k, :] = (ext[r, q, 1] + (r - 1.0)) * sigma
-        halo_rows[32 + k : 33 + k, :] = ext[r, q, 2]
-    halo_t[...] = jnp.transpose(halo_rows[...])
-    add_near(
-        halo_t, own_rows, total,
-        [(k, 16 + k, 32 + k, near_targets(r, q)) for k, (r, q) in enumerate(border)],
-    )
+    for side in (0, 1, -1):
+        for k, (dr, dc) in enumerate(directions):
+            if dc == -side:
+                halo[k].wait_recv()
+        cells = [
+            (r, q) for r, q in border if (q > COLS) - (q < 1) == side
+        ]
+        base = {0: 0, 1: 24, -1: 36}[side]
+        n = len(cells)
+        for k, (r, q) in enumerate(cells):
+            halo_rows[base + k : base + k + 1, :] = (ext[r, q, 0] + (q - 1.0)) * sigma
+            halo_rows[base + n + k : base + n + k + 1, :] = (ext[r, q, 1] + (r - 1.0)) * sigma
+            halo_rows[base + 2 * n + k : base + 2 * n + k + 1, :] = ext[r, q, 2]
+        rows = slice({0: 0, 1: 24, -1: 32}[side], {0: 24, 1: 40, -1: 48}[side])
+        halo_t[:, rows] = jnp.transpose(halo_rows[rows, :])
+        add_near(
+            halo_t, own_rows, total,
+            [
+                (base + k, base + n + k, base + 2 * n + k, near_targets(r, q))
+                for k, (r, q) in enumerate(cells)
+            ],
+        )
     for t in range(TILE):
         for i in range(2):
             near_uv[i, t : t + 1, :] = jnp.sum(total[2 * t + i], axis=0, keepdims=True) * near_scale
 
+    def down_copy(k, at_y=y, core=c):
+        return copy(final, final, down_send.at[k], down_recv, mesh_id(x, at_y, k % NZ, core))
+
+    first_chip = jnp.logical_and(x == 0, y == 0)
+    spared = jnp.logical_and(first_chip, c == 1)
+    stands_in = jnp.logical_and(first_chip, c == 0)
+
     @pl.when(is_root)
     def _():
-        for k in range(1, 2 * NX):
-            slot = lax.rem(c + k, 2) * NX + lax.rem(x + k // 2, NX)
-            copy(part.at[0], x_buf.at[slot], x_send.at[0], x_recv.at[slot], (tx, ty)).wait_recv()
-        for h in range(2):
-            final[h] = jnp.sum(x_buf[h * NX : (h + 1) * NX], axis=0)
-        for k in range(1, NZ):
-            down_copies[k - 1].start()
-
-    @pl.when(jnp.logical_not(is_root))
-    def _():
-        down_copies[0].wait_recv()
+        others = pl.ds(0, NX * NY - 1)
+        pltpu.make_async_copy(spread.at[others], spread.at[others], spread_recv).wait()
+
+    @pl.when(jnp.logical_and(in_plane, c == 0))
+    def _():
+        pltpu.make_async_copy(spread, spread, spread_recv).wait()
+
+    @pl.when(in_plane)
+    def _():
+        for k in range(NY):
+            final[k] = jnp.sum(spread[k * NX : (k + 1) * NX], axis=0)
+        @pl.when(stands_in)
+        def _():
+            for k in (1, 7, 2):
+                down_copy(k + NZ, 0, 1).start()
+
+        @pl.when(jnp.logical_not(spared))
+        def _():
+            for k in (1, 7, 2):
+                down_copy(k).start()
+
+        @pl.when(y != 0)
+        def _():
+            for k in (3, 4, 5, 6):
+                down_copy(k).start()
+
+        @pl.when(y == NY - 1)
+        def _():
+            for k in (3, 4, 5, 6):
+                down_copy(k + NZ, 0).start()
+
+    @pl.when(jnp.logical_not(in_plane))
+    def _():
+        down_copy(1).wait_recv()
 
     field_out[2:4] = off[...]
     field_out[4] = jnp.where(live, 1.0, 0.0)
 
-    modes = jnp.concatenate([final[0], final[1]], axis=0)
+    modes = jnp.concatenate([final[k] for k in range(NY)], axis=0)
     swapped = jnp.where(
         lax.rem(wide, 64) < HALF, pltpu.roll(modes, 96, 1), pltpu.roll(modes, 32, 1)
     )
@@ -387,17 +454,44 @@
 
     for sent in halo:
         sent.wait_send()
+    for k in range(1, NY):
+        part_copy(k).wait_send()
+
+    @pl.when(jnp.logical_not(is_root))
+    def _():
+        part_copy(0).wait_send()
 
     @pl.when(is_root)
     def _():
-        mate.wait_send()
-        for sent in y_copies + x_copies + down_copies:
-            sent.wait_send()
-
-    @pl.when(jnp.logical_not(is_root))
-    def _():
-        for h in range(2):
-            half_copy(h).wait_send()
+        for to_y in range(NY):
+            for k in range(1, 2 * NX):
+                spread_copy(k, to_y).wait_send()
+
+            @pl.when(y != to_y)
+            def _():
+                spread_copy(0, to_y).wait_send()
+
+    @pl.when(in_plane)
+    def _():
+        @pl.when(jnp.logical_not(spared))
+        def _():
+            for k in (1, 7, 2):
+                down_copy(k).wait_send()
+
+        @pl.when(stands_in)
+        def _():
+            for k in (1, 7, 2):
+                down_copy(k + NZ, 0, 1).wait_send()
+
+        @pl.when(y != 0)
+        def _():
+            for k in (3, 4, 5, 6):
+                down_copy(k).wait_send()
+
+        @pl.when(y == NY - 1)
+        def _():
+            for k in (3, 4, 5, 6):
+                down_copy(k + NZ, 0).wait_send()
 
 
 def per_device(offsets, circ, counts):
@@ -425,14 +519,12 @@
             pltpu.VMEM((192, TILE * SLOTS), jnp.bfloat16),
             pltpu.VMEM((128, TILE * SLOTS), jnp.bfloat16),
             pltpu.VMEM((2, HALF, 128), f32),
-            pltpu.VMEM((2, 16, 128), f32),
-            pltpu.VMEM((16, 16, 128), f32),
-            pltpu.VMEM((8, 16, 128), f32),
-            pltpu.VMEM((8, 16, 128), f32),
-            pltpu.VMEM((2, 16, 128), f32),
-            dma((8,)), dma((8,)), dma((2,)), dma((16,)), dma((8,)), dma((8,)), dma((8,)),
-            dma((8,)), dma((8,)), dma,
-            pltpu.SemaphoreType.REGULAR, dma((3,)),
+            pltpu.VMEM((NY, 4, 128), f32),
+            pltpu.VMEM((2 * NY * NZ, 4, 128), f32),
+            pltpu.VMEM((NY * NX, 4, 128), f32),
+            pltpu.VMEM((NY, 4, 128), f32),
+            dma((8,)), dma((8,)), dma((NY,)), dma, dma((NY, 2 * NX)), dma, dma((2 * NZ,)), dma,
+            dma((3,)), pltpu.SemaphoreType.REGULAR,
         ],
         compiler_params=pltpu.CompilerParams(
             collective_id=0, has_side_effects=True, vmem_limit_bytes=16 << 20

time: 30.2 us -> 28.8 us (0.954)
  the two profiles are of different devices: /device:TPU:1 before, /device:TPU:64 now
where the time goes in v4:
time: 28.8 us; the launch traced here: 28.6 us
  Pallas kernels  27.3 us (95%)
  between operations  0.65 us (2%)
  other arithmetic  0.62 us (2%)
    pallas_call x1, Pallas kernels, per_device(): pl.pallas_call(kernel, out_shape=shape, in_specs=[hbm, hbm, hbm], out_spe...  27.3 us
    add x1, other arithmetic, per_device(): return (velocity, field[2:4] + section_step * velocity)  0.61 us

profile of v4, /device:TPU:64, one launch (start us, length us, event | category | flops | bytes accessed | tf_op | source)
XLA Modules:
  0.0 28.6 jit_solution(13005721133492125492)
XLA Ops:
  0.6 27.3 %shard_map.50 = f32[5,8,128]{2,1,0:T(8,128)S(1)} custom-call(f32[2,8,128]{2,1,0:T(8,128)} %bitcast.7, f32[8,128]{1,0:T(8,128)} %bitcast.8, s32[2,4]{1,0:T(2,128)} %counts_hbm.1), custom_call_target="tpu_custom_call" | custom-call | tf_op jit(solution)/shard_map/pallas_call | solution.py:502
  28.0 0.6 %multiply_add_fusion = (f32[2,2,4,128]{3,2,1,0:T(4,128)}, f32[2,2,4,128]{3,2,1,0:T(4,128)}) fusion(f32[2,2,4,128]{3,2,1,0:T(4,128)S(1)} %bitcast.6, f32[2,2,4,128]{3,2,1,0:T(4,128)S(1)} %bitcast.5, pred[2,4,128]{2,1,0:T(4,128)(4,1)S(1)} %bitcast.9), kind=kLoop, calls=%fused_computation | loop fusion | flops 6144 | bytes 33792 | tf_op jit(solution)/shard_map/add | solution.py:540
  (2 shorter events, 0.0 us)

commit v5 on v4

--- a/solution.py
+++ b/solution.py
@@ -23,6 +23,15 @@
 alpha = screen / math.log(2.0)
 sigma = math.sqrt(alpha)
 near_scale = CELLS / two_pi * sigma
+ROWS_FIRST = (0, 1, 2, 3, 7, 6, 5, 4)
+SPREAD_ORDER = tuple(
+    (x, y, c)
+    for rows in ((0, 1, 2), (3, 7, 6, 5, 4))
+    for columns in ((0,), (1, 2, 3))
+    for y in rows
+    for x in columns
+    for c in (1, 0)
+)
 directions = tuple((dr, dc) for dr in (-1, 0, 1) for dc in (-1, 0, 1) if (dr, dc) != (0, 0))
 
 
@@ -144,6 +153,8 @@
     x, y, z, c = fan(tx, ty)
     in_plane = z == 0
     is_root = jnp.logical_and(in_plane, c == 1)
+    is_guest = jnp.logical_and(jnp.logical_and(x == 0, y == 0), z == 1)
+    listens = jnp.logical_or(in_plane, is_guest)
 
     def host_row(row):
         return jnp.where(jnp.logical_or(row == 3, row == 5), 4, row)
@@ -183,7 +194,7 @@
 
     own_slot = (y * NZ + z) * 2 + c
 
-    @pl.when(in_plane)
+    @pl.when(listens)
     def _():
         def to_roots(k, carry):
             greet(mesh_id(lax.rem(x + 1 + lax.div(k, NY), NX), lax.rem(y + k, NY), 0, 1))
@@ -254,7 +265,7 @@
 
     @pl.when(is_root)
     def _():
-        pl.semaphore_wait(barrier, (NY - 1) + 2 * NY * (NX - 1))
+        pl.semaphore_wait(barrier, (NY - 1) + 2 * NY * (NX - 1) + jnp.where(x == 0, 0, 2))
 
     def part_copy(k):
         at = lax.rem(y + k, NY)
@@ -324,11 +335,29 @@
         )
         halo[-1].start()
 
-    def spread_copy(k, to_y):
+    def spread_copy(to_x, to_y, to_c):
         return copy(
-            spread.at[y * NX + x], spread.at[y * NX + x], spread_send.at[to_y, k], spread_recv,
-            mesh_id(lax.rem(x + k // 2, NX), to_y, 0, lax.rem(c + k, 2)),
-        )
+            spread.at[y * NX + x], spread.at[y * NX + x],
+            spread_send.at[to_y, 2 * to_x + to_c], spread_recv, mesh_id(to_x, to_y, 0, to_c),
+        )
+
+    def each_spread(act):
+        for at, (to_x, to_y, to_c) in enumerate(SPREAD_ORDER):
+            if at == 2:
+                for core in range(2):
+                    act(
+                        copy(
+                            spread.at[y * NX + x], spread.at[y * NX + x],
+                            spread_send.at[NY, core], spread_recv, mesh_id(0, 0, 1, core),
+                        )
+                    )
+            if to_c == 0:
+                act(spread_copy(to_x, to_y, to_c))
+            else:
+
+                @pl.when(jnp.logical_or(x != to_x, y != to_y))
+                def _(to_x=to_x, to_y=to_y, to_c=to_c):
+                    act(spread_copy(to_x, to_y, to_c))
 
     @pl.when(is_root)
     def _():
@@ -336,13 +365,7 @@
         others = pl.ds(0, 2 * NY * NZ - 1)
         pltpu.make_async_copy(gathered.at[others], gathered.at[others], part_recv).wait()
         spread[y * NX + x] = jnp.sum(gathered[...], axis=0)
-        for to_y in (0, 1, 2, 3, 7, 6, 5, 4):
-            for k in range(1, 2 * NX):
-                spread_copy(k, to_y).start()
-
-            @pl.when(y != to_y)
-            def _():
-                spread_copy(0, to_y).start()
+        each_spread(lambda sent: sent.start())
 
     border = [
         (r, q) for r in range(ROWS + 2) for q in range(COLS + 2)
@@ -378,7 +401,6 @@
         return copy(final, final, down_send.at[k], down_recv, mesh_id(x, at_y, k % NZ, core))
 
     first_chip = jnp.logical_and(x == 0, y == 0)
-    spared = jnp.logical_and(first_chip, c == 1)
     stands_in = jnp.logical_and(first_chip, c == 0)
 
     @pl.when(is_root)
@@ -386,20 +408,24 @@
         others = pl.ds(0, NX * NY - 1)
         pltpu.make_async_copy(spread.at[others], spread.at[others], spread_recv).wait()
 
-    @pl.when(jnp.logical_and(in_plane, c == 0))
+    @pl.when(jnp.logical_and(listens, jnp.logical_not(is_root)))
     def _():
         pltpu.make_async_copy(spread, spread, spread_recv).wait()
 
-    @pl.when(in_plane)
+    @pl.when(listens)
     def _():
         for k in range(NY):
             final[k] = jnp.sum(spread[k * NX : (k + 1) * NX], axis=0)
+
+    @pl.when(in_plane)
+    def _():
         @pl.when(stands_in)
         def _():
-            for k in (1, 7, 2):
+            for k in (2, 7):
                 down_copy(k + NZ, 0, 1).start()
-
-        @pl.when(jnp.logical_not(spared))
+                down_copy(k).start()
+
+        @pl.when(jnp.logical_not(first_chip))
         def _():
             for k in (1, 7, 2):
                 down_copy(k).start()
@@ -414,7 +440,7 @@
             for k in (3, 4, 5, 6):
                 down_copy(k + NZ, 0).start()
 
-    @pl.when(jnp.logical_not(in_plane))
+    @pl.when(jnp.logical_not(listens))
     def _():
         down_copy(1).wait_recv()
 
@@ -463,25 +489,20 @@
 
     @pl.when(is_root)
     def _():
-        for to_y in range(NY):
-            for k in range(1, 2 * NX):
-                spread_copy(k, to_y).wait_send()
-
-            @pl.when(y != to_y)
-            def _():
-                spread_copy(0, to_y).wait_send()
+        each_spread(lambda sent: sent.wait_send())
 
     @pl.when(in_plane)
     def _():
-        @pl.when(jnp.logical_not(spared))
+        @pl.when(jnp.logical_not(first_chip))
         def _():
             for k in (1, 7, 2):
                 down_copy(k).wait_send()
 
         @pl.when(stands_in)
         def _():
-            for k in (1, 7, 2):
+            for k in (2, 7):
                 down_copy(k + NZ, 0, 1).wait_send()
+                down_copy(k).wait_send()
 
         @pl.when(y != 0)
         def _():
@@ -523,7 +544,7 @@
             pltpu.VMEM((2 * NY * NZ, 4, 128), f32),
             pltpu.VMEM((NY * NX, 4, 128), f32),
             pltpu.VMEM((NY, 4, 128), f32),
-            dma((8,)), dma((8,)), dma((NY,)), dma, dma((NY, 2 * NX)), dma, dma((2 * NZ,)), dma,
+            dma((8,)), dma((8,)), dma((NY,)), dma, dma((NY + 1, 2 * NX)), dma, dma((2 * NZ,)), dma,
             dma((3,)), pltpu.SemaphoreType.REGULAR,
         ],
         compiler_params=pltpu.CompilerParams(

time: 28.8 us -> 28 us (0.972)
  the two profiles are of different devices: /device:TPU:64 before, /device:TPU:1 now
where the time goes in v5:
time: 28 us; the launch traced here: 27.8 us
  Pallas kernels  26.6 us (95%)
  between operations  0.65 us (2%)
  other arithmetic  0.62 us (2%)
    pallas_call x1, Pallas kernels, per_device(): pl.pallas_call(kernel, out_shape=shape, in_specs=[hbm, hbm, hbm], out_spe...  26.6 us
    add x1, other arithmetic, per_device(): return (velocity, field[2:4] + section_step * velocity)  0.61 us

profile of v5, /device:TPU:1, one launch (start us, length us, event | category | flops | bytes accessed | tf_op | source)
XLA Modules:
  0.0 27.8 jit_solution(9479467346405088190)
XLA Ops:
  0.6 26.6 %shard_map.50 = f32[5,8,128]{2,1,0:T(8,128)S(1)} custom-call(f32[2,8,128]{2,1,0:T(8,128)} %bitcast.7, f32[8,128]{1,0:T(8,128)} %bitcast.8, s32[2,4]{1,0:T(2,128)} %counts_hbm.1), custom_call_target="tpu_custom_call" | custom-call | tf_op jit(solution)/shard_map/pallas_call | solution.py:523
  27.2 0.6 %multiply_add_fusion = (f32[2,2,4,128]{3,2,1,0:T(4,128)}, f32[2,2,4,128]{3,2,1,0:T(4,128)}) fusion(f32[2,2,4,128]{3,2,1,0:T(4,128)S(1)} %bitcast.6, f32[2,2,4,128]{3,2,1,0:T(4,128)S(1)} %bitcast.5, pred[2,4,128]{2,1,0:T(4,128)(4,1)S(1)} %bitcast.9), kind=kLoop, calls=%fused_computation | loop fusion | flops 6144 | bytes 33792 | tf_op jit(solution)/shard_map/add | solution.py:561
  (2 shorter events, 0.0 us)

commit v6 on v5

--- a/solution.py
+++ b/solution.py
@@ -72,6 +72,18 @@
     return 1.0 - 2.0 * sine * sine, 2.0 * sine * cosine
 
 
+def wave_tables(position):
+    few = lax.broadcasted_iota(jnp.int32, (8, SLOTS), 0).astype(jnp.float32)
+    cos_few, sin_few = cos_sin(few * position)
+    cos_step, sin_step = cos_sin(few * (8.0 * position))
+    cosines, sines = [cos_few], [sin_few]
+    for k in range(1, HALF // 8):
+        cos_k, sin_k = cos_step[k : k + 1], sin_step[k : k + 1]
+        cosines.append(cos_k * cos_few - sin_k * sin_few)
+        sines.append(sin_k * cos_few + cos_k * sin_few)
+    return jnp.concatenate(cosines, axis=0), jnp.concatenate(sines, axis=0)
+
+
 def split(value):
     high = value.astype(jnp.bfloat16)
     return high, (value - high.astype(jnp.float32)).astype(jnp.bfloat16)
@@ -227,7 +239,6 @@
     cell_col = lax.rem(row_of, COLS).astype(jnp.float32)
     own_rows[2 * TILE : 3 * TILE, :] = strength
 
-    wave = lax.broadcasted_iota(jnp.int32, (HALF, SLOTS), 0).astype(jnp.float32)
     first_col = (ty * COLS).astype(jnp.float32)
     first_row = (tx * ROWS).astype(jnp.float32)
     for cell in range(TILE):
@@ -235,13 +246,13 @@
         pos_x = (off[0, cell : cell + 1, :] + (first_col + cell % COLS)) * (1.0 / CELLS)
         pos_y = (off[1, cell : cell + 1, :] + (first_row + cell // COLS)) * (1.0 / CELLS)
         weight = own_rows[2 * TILE + cell : 2 * TILE + cell + 1, :]
-        for at, table in enumerate(cos_sin(wave * pos_x)):
+        for at, table in enumerate(wave_tables(pos_x)):
             rows = slice(at * HALF, (at + 1) * HALF)
             tab_x[rows, lanes] = table
             high, low = split(table * weight)
             sided[rows, lanes] = high
             sided[64 + at * HALF : 64 + (at + 1) * HALF, lanes] = low
-        for at, table in enumerate(cos_sin(wave * pos_y)):
+        for at, table in enumerate(wave_tables(pos_y)):
             high, low = split(table)
             tab_y[at * HALF : (at + 1) * HALF, lanes] = high
             tab_y[64 + at * HALF : 64 + (at + 1) * HALF, lanes] = high
@@ -364,7 +375,14 @@
         gathered[own_slot] = part[y]
         others = pl.ds(0, 2 * NY * NZ - 1)
         pltpu.make_async_copy(gathered.at[others], gathered.at[others], part_recv).wait()
-        spread[y * NX + x] = jnp.sum(gathered[...], axis=0)
+        some = [gathered[k : k + 16] for k in range(0, 2 * NY * NZ, 16)]
+        while len(some) > 1:
+            some = [some[k] + some[k + 1] for k in range(0, len(some), 2)]
+        whole = some[0]
+        while whole.shape[0] > 1:
+            half = whole.shape[0] // 2
+            whole = whole[:half] + whole[half:]
+        spread[y * NX + x] = whole[0]
         each_spread(lambda sent: sent.start())
 
     border = [

time: 28 us -> 27.9 us (level)
  no operation moved by 1% of the time
where the time goes in v6:
time: 27.9 us; the launch traced here: 27.7 us
  Pallas kernels  26.5 us (95%)
  between operations  0.65 us (2%)
  other arithmetic  0.62 us (2%)
    pallas_call x1, Pallas kernels, per_device(): pl.pallas_call(kernel, out_shape=shape, in_specs=[hbm, hbm, hbm], out_spe...  26.5 us
    add x1, other arithmetic, per_device(): return (velocity, field[2:4] + section_step * velocity)  0.61 us

profile of v6, /device:TPU:1, one launch (start us, length us, event | category | flops | bytes accessed | tf_op | source)
XLA Modules:
  0.0 27.7 jit_solution(13340278393435564913)
XLA Ops:
  0.6 26.5 %shard_map.50 = f32[5,8,128]{2,1,0:T(8,128)S(1)} custom-call(f32[2,8,128]{2,1,0:T(8,128)} %bitcast.7, f32[8,128]{1,0:T(8,128)} %bitcast.8, s32[2,4]{1,0:T(2,128)} %counts_hbm.1), custom_call_target="tpu_custom_call" | custom-call | tf_op jit(solution)/shard_map/pallas_call | solution.py:541
  27.1 0.6 %multiply_add_fusion = (f32[2,2,4,128]{3,2,1,0:T(4,128)}, f32[2,2,4,128]{3,2,1,0:T(4,128)}) fusion(f32[2,2,4,128]{3,2,1,0:T(4,128)S(1)} %bitcast.6, f32[2,2,4,128]{3,2,1,0:T(4,128)S(1)} %bitcast.5, pred[2,4,128]{2,1,0:T(4,128)(4,1)S(1)} %bitcast.9), kind=kLoop, calls=%fused_computation | loop fusion | flops 6144 | bytes 33792 | tf_op jit(solution)/shard_map/add | solution.py:579
  (2 shorter events, 0.0 us)

commit v7 on v6

--- a/solution.py
+++ b/solution.py
@@ -298,6 +298,8 @@
         send_parts()
         part_copy(0).start()
 
+    field_out[2:4] = off[...]
+    field_out[4] = jnp.where(live, 1.0, 0.0)
     own_rows[0:TILE, :] = (off_x + cell_col) * sigma
     own_rows[TILE : 2 * TILE, :] = (off_y + cell_row) * sigma
     own_t[...] = jnp.transpose(own_rows[...])
@@ -461,9 +463,6 @@
     @pl.when(jnp.logical_not(listens))
     def _():
         down_copy(1).wait_recv()
-
-    field_out[2:4] = off[...]
-    field_out[4] = jnp.where(live, 1.0, 0.0)
 
     modes = jnp.concatenate([final[k] for k in range(NY)], axis=0)
     swapped = jnp.where(

time: 27.9 us -> 27.9 us (level)
  no operation moved by 1% of the time
where the time goes in v7:
time: 27.9 us; the launch traced here: 27.7 us
  Pallas kernels  26.5 us (95%)
  between operations  0.65 us (2%)
  other arithmetic  0.62 us (2%)
    pallas_call x1, Pallas kernels, per_device(): pl.pallas_call(kernel, out_shape=shape, in_specs=[hbm, hbm, hbm], out_spe...  26.5 us
    add x1, other arithmetic, per_device(): return (velocity, field[2:4] + section_step * velocity)  0.61 us

profile of v7, /device:TPU:1, one launch (start us, length us, event | category | flops | bytes accessed | tf_op | source)
XLA Modules:
  0.0 27.7 jit_solution(9168121268318839478)
XLA Ops:
  0.6 26.5 %shard_map.50 = f32[5,8,128]{2,1,0:T(8,128)S(1)} custom-call(f32[2,8,128]{2,1,0:T(8,128)} %bitcast.7, f32[8,128]{1,0:T(8,128)} %bitcast.8, s32[2,4]{1,0:T(2,128)} %counts_hbm.1), custom_call_target="tpu_custom_call" | custom-call | tf_op jit(solution)/shard_map/pallas_call | solution.py:540
  27.1 0.6 %multiply_add_fusion = (f32[2,2,4,128]{3,2,1,0:T(4,128)}, f32[2,2,4,128]{3,2,1,0:T(4,128)}) fusion(f32[2,2,4,128]{3,2,1,0:T(4,128)S(1)} %bitcast.6, f32[2,2,4,128]{3,2,1,0:T(4,128)S(1)} %bitcast.5, pred[2,4,128]{2,1,0:T(4,128)(4,1)S(1)} %bitcast.9), kind=kLoop, calls=%fused_computation | loop fusion | flops 6144 | bytes 33792 | tf_op jit(solution)/shard_map/add | solution.py:578
  (2 shorter events, 0.0 us)
